TPU v7x, 512 devices: a whole 4x4x16 slice. The times are simulated.
512 devices in a mesh: box: 512 (over z, y, x, core).
Axes of the slice: x: 4, y: 4, z: 16, core: 2. Of those that a mesh axis runs over, the one named last changes fastest.
Arguments:
- cell_state: float32 [1024, 5, 32, 1024], P('box'), as said below
- swap_slots: int32 [512], P('box'), may hold values from 0 to 1, as said below
- neighbours: int32 [1024, 3], P('box'), may hold values from -1 to 1023, as said below
Outputs:
- new_state: float32 [1024, 5, 32, 1024], P('box')
Inputs may be any that keep to these rules, and one draw needn't show every extreme that they name: `swap_slots`: each device names one of its 2 slots. `neighbours`: after the swap, device d holds the boxes of first-dimension layer d of a domain 512 layers long and two boxes wide in the second dimension; the lower first-dimension neighbour of a slot lies on device d - 1, the upper on device d + 1, the box beside in the second dimension on device d itself; -1 marks the two ends of the first dimension. `cell_state`: density, pressure and internal energy of every cell are positive.
All inputs are finite; a program needn't handle non-finite values.
Results may differ from a plain program's by a relative error of at most 0.0003.
Values sent between devices are 32-bit elements; how exact they have to be, the bound alone decides.
No kernel may reach another device: no remote copies, remote signals or barrier semaphores. Data moves between devices by JAX's collectives and lax.ppermute only.
A program may use at most 64 MiB of HBM per device.

v0:
```python
import jax
import jax.numpy as jnp
from jax import lax
from jax.sharding import PartitionSpec as P

BZC = 32
GHOST = 4
RIEMANN_ITERS = 3


EOS_LINEAR = 0.4
EOS_QUAD = 0.1
COURANT = 0.4


def from_behind(value, axis, steps):
    count = lax.axis_size(axis)
    initial, last = (max(0, -steps), min(count, count - steps))
    return lax.ppermute(value, axis, [(source, source + steps) for source in range(initial, last)])


def from_partner(shard, axis, distance):
    return lax.ppermute(shard, axis, [(i, i ^ 1 << distance) for i in range(lax.axis_size(axis))])


def layers(values, start, stop, sweep_axis, unit):
    return lax.slice_in_dim(values, start * unit, stop * unit, axis=sweep_axis)


def roll_cells(values, offset_by):
    position = lax.broadcasted_iota(jnp.int32, values.shape, values.ndim - 1) % BZC
    inside = jnp.roll(values, -offset_by, axis=values.ndim - 1)
    if offset_by > 0:
        wrapped = jnp.roll(values, BZC - offset_by, axis=values.ndim - 1)
        return jnp.where(position + offset_by < BZC, inside, wrapped)
    wrapped = jnp.roll(values, -offset_by - BZC, axis=values.ndim - 1)
    return jnp.where(position + offset_by >= 0, inside, wrapped)


def minmod(first, second):
    return 0.5 * (jnp.sign(first) + jnp.sign(second)) * jnp.minimum(jnp.abs(first), jnp.abs(second))


def primitives(conserved):
    density = jnp.maximum(conserved[0], 0.05)
    velocity = conserved[1:4] / density
    internal = jnp.maximum(
        conserved[4] / density - 0.5 * jnp.sum(velocity * velocity, axis=0), 0.05
    )
    pressure = EOS_LINEAR * density * internal + EOS_QUAD * density * density
    return jnp.concatenate([density[None], velocity, pressure[None]], axis=0)


def fastest(conserved):
    prims = primitives(conserved)
    density = prims[0]
    sound = jnp.sqrt((EOS_QUAD * density * density + (1.0 + EOS_LINEAR) * prims[4]) / density)
    return jnp.max(jnp.abs(prims[1]) + jnp.abs(prims[2]) + jnp.abs(prims[3]) + 3.0 * sound)


def face_states(prims, sweep_axis, unit, component):
    length = prims.shape[sweep_axis] // unit
    inner = length - 8
    before = layers(prims, 0, length - 3, sweep_axis, unit)
    centre_a = layers(prims, 1, length - 2, sweep_axis, unit)
    centre_b = layers(prims, 2, length - 1, sweep_axis, unit)
    after_b = layers(prims, 3, length, sweep_axis, unit)
    faces = 7.0 / 12.0 * (centre_a + centre_b) - 1.0 / 12.0 * (before + after_b)
    faces = jnp.clip(faces, jnp.minimum(centre_a, centre_b), jnp.maximum(centre_a, centre_b))
    centre = layers(prims, 3, inner + 5, sweep_axis, unit)
    left_edge = layers(faces, 1, inner + 3, sweep_axis, unit)
    right_edge = layers(faces, 2, inner + 4, sweep_axis, unit)
    pressure = prims[4:5]
    normal = prims[component : component + 1]
    near_diff = layers(pressure, 3, length - 1, sweep_axis, unit) - layers(
        pressure, 1, length - 3, sweep_axis, unit
    )
    far_diff = layers(pressure, 4, length, sweep_axis, unit) - layers(
        pressure, 0, length - 4, sweep_axis, unit
    )
    far_sum = layers(pressure, 4, length, sweep_axis, unit) + layers(
        pressure, 0, length - 4, sweep_axis, unit
    )
    steepness = jnp.abs(near_diff) / (jnp.abs(far_diff) + 0.1 * far_sum)
    squeeze = jnp.maximum(
        layers(normal, 1, length - 3, sweep_axis, unit)
        - layers(normal, 3, length - 1, sweep_axis, unit),
        0.0,
    )
    shock = jnp.clip((steepness - 0.75) * 4.0, 0.0, 1.0) * squeeze / (squeeze + 0.2)
    widest = jnp.maximum(
        jnp.maximum(
            layers(shock, 0, inner + 2, sweep_axis, unit),
            layers(shock, 1, inner + 3, sweep_axis, unit),
        ),
        layers(shock, 2, inner + 4, sweep_axis, unit),
    )
    flatten = 1.0 - widest
    down_part = minmod(centre - left_edge, 2.0 * (right_edge - centre))
    up_part = minmod(right_edge - centre, 2.0 * (centre - left_edge))
    lower_val = centre - flatten * down_part
    upper_val = centre + flatten * up_part
    return (
        layers(upper_val, 0, inner + 1, sweep_axis, unit),
        layers(lower_val, 1, inner + 2, sweep_axis, unit),
    )


def periodic_states(prims, component):
    before = roll_cells(prims, -1)
    after_one = roll_cells(prims, 1)
    after_two = roll_cells(prims, 2)
    faces = 7.0 / 12.0 * (prims + after_one) - 1.0 / 12.0 * (before + after_two)
    faces = jnp.clip(faces, jnp.minimum(prims, after_one), jnp.maximum(prims, after_one))
    left_edge = roll_cells(faces, -1)
    pressure = prims[4:5]
    normal = prims[component : component + 1]
    near_diff = roll_cells(pressure, 1) - roll_cells(pressure, -1)
    far_diff = roll_cells(pressure, 2) - roll_cells(pressure, -2)
    far_sum = roll_cells(pressure, 2) + roll_cells(pressure, -2)
    steepness = jnp.abs(near_diff) / (jnp.abs(far_diff) + 0.1 * far_sum)
    squeeze = jnp.maximum(roll_cells(normal, -1) - roll_cells(normal, 1), 0.0)
    shock = jnp.clip((steepness - 0.75) * 4.0, 0.0, 1.0) * squeeze / (squeeze + 0.2)
    widest = jnp.maximum(jnp.maximum(roll_cells(shock, -1), shock), roll_cells(shock, 1))
    flatten = 1.0 - widest
    down_part = minmod(prims - left_edge, 2.0 * (faces - prims))
    up_part = minmod(faces - prims, 2.0 * (prims - left_edge))
    lower_val = prims - flatten * down_part
    upper_val = prims + flatten * up_part
    return (roll_cells(upper_val, -1), lower_val)


def wave_side(prims):
    density = prims[0]
    pressure = prims[4]
    internal = jnp.maximum((pressure - EOS_QUAD * density * density) / (EOS_LINEAR * density), 0.05)
    impedance = jnp.sqrt(density * (EOS_QUAD * density * density + (1.0 + EOS_LINEAR) * pressure))
    gamma_eff = 1.0 + EOS_LINEAR + EOS_QUAD * density * density / pressure
    growth = (gamma_eff + 1.0) / (2.0 * gamma_eff)
    return (density, pressure, internal, impedance, growth)


def riemann(left_state, right_state, sweep_axis):
    dens_l, pres_l, int_l, imp_l, grow_l = wave_side(left_state)
    dens_r, pres_r, int_r, imp_r, grow_r = wave_side(right_state)
    vel_l = left_state[sweep_axis]
    vel_r = right_state[sweep_axis]
    floor_p = 0.1 * jnp.minimum(pres_l, pres_r)
    p_star = (imp_r * pres_l + imp_l * pres_r + imp_l * imp_r * (vel_l - vel_r)) / (imp_l + imp_r)
    p_star = jnp.maximum(p_star, floor_p)

    def speeds(guess):
        wave_l = imp_l * jnp.sqrt(1.0 + grow_l * (guess / pres_l - 1.0))
        wave_r = imp_r * jnp.sqrt(1.0 + grow_r * (guess / pres_r - 1.0))
        return (wave_l, wave_r)

    for sweep_turn in range(RIEMANN_ITERS):
        wave_l, wave_r = speeds(p_star)
        star_l = vel_l - (p_star - pres_l) / wave_l
        star_r = vel_r + (p_star - pres_r) / wave_r
        slope_l = 2.0 * wave_l**3 / (wave_l * wave_l + imp_l * imp_l)
        slope_r = 2.0 * wave_r**3 / (wave_r * wave_r + imp_r * imp_r)
        p_star = jnp.maximum(
            p_star - slope_l * slope_r * (star_r - star_l) / (slope_l + slope_r), floor_p
        )
    wave_l, wave_r = speeds(p_star)
    star_l = vel_l - (p_star - pres_l) / wave_l
    star_r = vel_r + (p_star - pres_r) / wave_r
    u_star = (wave_l * star_l + wave_r * star_r) / (wave_l + wave_r)
    vol_l = 1.0 / dens_l - (p_star - pres_l) / (wave_l * wave_l)
    vol_r = 1.0 / dens_r - (p_star - pres_r) / (wave_r * wave_r)
    inner_l = jnp.maximum(int_l + 0.5 * (p_star + pres_l) * (1.0 / dens_l - vol_l), 0.1 * int_l)
    inner_r = jnp.maximum(int_r + 0.5 * (p_star + pres_r) * (1.0 / dens_r - vol_r), 0.1 * int_r)
    upwind = u_star >= 0.0
    dens_star = jnp.where(upwind, 1.0 / vol_l, 1.0 / vol_r)
    inner_star = jnp.where(upwind, inner_l, inner_r)
    mass = dens_star * u_star
    kinetic = u_star * u_star
    momenta = []
    for component in range(1, 4):
        if component == sweep_axis:
            momenta.append(mass * u_star + p_star)
        else:
            carried = jnp.where(upwind, left_state[component], right_state[component])
            kinetic = kinetic + carried * carried
            momenta.append(mass * carried)
    energy = u_star * (dens_star * (inner_star + 0.5 * kinetic) + p_star)
    return jnp.stack([mass] + momenta + [energy], axis=0)


def rate(conserved, low_x, high_x, low_y, high_y, ratio):
    depth = conserved.shape[1]
    side_rows = conserved.shape[2] // BZC
    extended_x = jnp.concatenate([low_x, conserved, high_x], axis=1)
    extended_y = jnp.concatenate([low_y, conserved, high_y], axis=2)
    tendency = jnp.zeros_like(conserved)
    left_state, right_state = face_states(primitives(extended_x), 1, 1, 1)
    fluxes = riemann(left_state, right_state, 1)
    tendency = tendency - ratio * (
        layers(fluxes, 1, depth + 1, 1, 1) - layers(fluxes, 0, depth, 1, 1)
    )
    left_state, right_state = face_states(primitives(extended_y), 2, BZC, 2)
    fluxes = riemann(left_state, right_state, 2)
    tendency = tendency - ratio * (
        layers(fluxes, 1, side_rows + 1, 2, BZC) - layers(fluxes, 0, side_rows, 2, BZC)
    )
    left_state, right_state = periodic_states(primitives(conserved), 3)
    fluxes = riemann(left_state, right_state, 3)
    tendency = tendency - ratio * (roll_cells(fluxes, 1) - fluxes)
    return tendency


def near_faces(box_data):
    nearby = []
    for offset_by in (1, -1):
        nearby.append(from_behind(box_data, "box", offset_by))
    return (nearby[0][:, :, -GHOST:], nearby[1][:, :, :GHOST])


def local_rate(box_data, neighbours, own_start, ratio):
    slots = box_data.shape[0]
    side_span = GHOST * BZC
    below, above = near_faces(box_data)
    lower = neighbours[:, 0]
    upper = neighbours[:, 1]
    beside = neighbours[:, 2]
    from_lower = jnp.take(below, jnp.clip(lower - own_start + slots, 0, slots - 1), axis=0)
    from_upper = jnp.take(above, jnp.clip(upper - own_start - slots, 0, slots - 1), axis=0)
    edge_low = jnp.broadcast_to(box_data[:, :, :1], from_lower.shape)
    edge_high = jnp.broadcast_to(box_data[:, :, -1:], from_upper.shape)
    low_x = jnp.where((lower < 0)[:, None, None, None], edge_low, from_lower)
    high_x = jnp.where((upper < 0)[:, None, None, None], edge_high, from_upper)
    side_index = jnp.clip(beside - own_start, 0, slots - 1)
    low_y = jnp.take(box_data[..., -side_span:], side_index, axis=0)
    high_y = jnp.take(box_data[..., :side_span], side_index, axis=0)

    def unpack_rate(bundle):
        return rate(bundle[0], bundle[1], bundle[2], bundle[3], bundle[4], ratio)

    return lax.map(unpack_rate, (box_data, low_x, high_x, low_y, high_y))


def body(cell_state, swap_slots, neighbours):
    slots = cell_state.shape[0]
    chosen_slot = swap_slots[0]
    outgoing = lax.dynamic_index_in_dim(cell_state, chosen_slot, 0, keepdims=False)
    half_bit = lax.axis_size("box").bit_length() - 2
    incoming = from_partner(outgoing, "box", half_bit)
    chosen = jnp.arange(slots, dtype=jnp.int32) == chosen_slot
    box_data = jnp.where(chosen[:, None, None, None], incoming[None], cell_state)
    local_fast = jnp.max(lax.map(fastest, box_data))
    ratio = COURANT / lax.pmax(local_fast, "box")
    own_start = lax.axis_index("box") * slots
    first = box_data + local_rate(box_data, neighbours, own_start, ratio)
    return 0.5 * (box_data + first + local_rate(first, neighbours, own_start, ratio))


def solution(mesh):
    in_specs = (P("box", None, None, None), P("box"), P("box", None))
    out_specs = P("box", None, None, None)
    return jax.shard_map(body, mesh=mesh, in_specs=in_specs, out_specs=out_specs, check_vma=False)
```

profile of v0, /device:TPU:32, one launch (start us, length us, event | category | flops | bytes accessed | tf_op | source)
XLA Modules:
  0.0 365.3 jit_solution(13003280721601407414)
XLA Ops:
  0.8 1.1 dynamic-slice_bitcast_fusion.16
  1.9 14.8 %collective-permute-start = (f32[5,32,1024]{2,1,0:T(8,128)S(1)}, f32[5,32,1024]{2,1,0:T(8,128)S(1)}, u32[]{:S(2)}, u32[]{:S(2)}) collective-permute-start(f32[5,32,1024]{2,1,0:T(8,128)S(1)} %dynamic-slice_bitcast_fusion.16), channel_id=1, source_target_pairs={{0,256},{1,257},{2,258},{3,259},{4,260},{5,261},{6,262},{7,263},{8... | collective-permute-start | bytes 1966088 | tf_op jit(solution)/shard_map/ppermute | solution.py:23
  17.3 56.8 %collective-permute-done = f32[5,32,1024]{2,1,0:T(8,128)S(1)} collective-permute-done((f32[5,32,1024]{2,1,0:T(8,128)S(1)}, f32[5,32,1024]{2,1,0:T(8,128)S(1)}, u32[]{:S(2)}, u32[]{:S(2)}) %collective-permute-start) | collective-permute-done | bytes 655392 | tf_op jit(solution)/shard_map/ppermute | solution.py:23
  74.1 1.3 broadcast_select_fusion
  75.4 1.9 collective-permute-start.2
  77.3 2.4 collective-permute-start.1
  79.7 9.0 %while.36 = (s32[]{:T(128)}, f32[2]{0:T(128)S(1)}, f32[2,5,32,1024]{3,2,1,0:T(8,128)}, s32[]{:T(128)}, s32[]{:T(128)}, /*index=5*/s32[]{}, s32[]{}) while((s32[]{:T(128)}, f32[2]{0:T(128)S(1)}, f32[2,5,32,1024]{3,2,1,0:T(8,128)}, s32[]{:T(128)}, s32[]{:T(128)}, /*index=5*/s32[]{}, s32[]{}) %tuple.359), condition=%wide.region_3.6_spmd, body=%wide.region_0.5_spmd.sunk | while | flops 983043 | bytes 2097289 | solution.py:251
  81.7 1.7 fusion.350
  86.2 1.7 fusion.350
  89.3 111.6 %pmax.7 = f32[]{:T(128)} all-reduce(f32[]{:T(128)} %reduce_max.18), channel_id=1, replica_groups=mesh['box'=512] {'box'}, use_global_device_ids=true, to_apply=%region_5.8 | all-reduce | flops 1 | bytes 8 | tf_op jit(solution)/shard_map/pmax | solution.py:252
  203.1 1.1 fusion.307
  210.0 1.2 broadcast.4793.clone
  211.2 65.6 %while.37 = (s32[]{:T(128)}, f32[2,5,32,1024]{3,2,1,0:T(8,128)}, f32[]{:T(128)}, f32[2,5,4,1024]{3,2,1,0:T(4,128)}, f32[2,5,32,1024]{3,2,1,0:T(8,128)}, /*index=...) while((s32[]{:T(128)}, f32[2,5,32,1024]{3,2,1,0:T(8,128)}, ...), condition=%wide.region_10.13_spmd, body=%wide.region_6.12_spmd.sunk | while | flops 59260928 | bytes 99735536 | solution.py:240
  231.1 1.1 multiply_add_fusion.50
  232.8 1.3 constant_dynamic-update-slice_fusion.14
  235.1 1.1 dynamic-slice_bitcast_fusion.24
  238.2 1.4 multiply_add_fusion.49
  239.7 1.7 constant_dynamic-update-slice_fusion.13
  244.5 1.4 multiply_add_fusion.48
  245.9 1.6 constant_dynamic-update-slice_fusion.12
  257.5 1.1 multiply_add_fusion.50
  259.3 1.3 constant_dynamic-update-slice_fusion.14
  261.5 1.1 dynamic-slice_bitcast_fusion.24
  264.6 1.4 multiply_add_fusion.49
  266.1 1.7 constant_dynamic-update-slice_fusion.13
  270.9 1.4 multiply_add_fusion.48
  272.3 1.6 constant_dynamic-update-slice_fusion.12
  276.9 1.7 fusion.308
  278.5 2.1 collective-permute-start.4
  280.6 2.2 collective-permute-start.3
  285.1 10.7 %collective-permute-done.4 = f32[2,5,32,1024]{3,2,1,0:T(8,128)} collective-permute-done((f32[2,5,32,1024]{3,2,1,0:T(8,128)S(1)}, f32[2,5,32,1024]{3,2,1,0:T(8,128)}, u32[]{:S(2)}, u32[]{:S(2)}) %collective-permute-start.4) | collective-permute-done | bytes 1310752 | tf_op jit(solution)/shard_map/ppermute | solution.py:19
  297.4 6.5 %collective-permute-done.3 = f32[2,5,32,1024]{3,2,1,0:T(8,128)} collective-permute-done((f32[2,5,32,1024]{3,2,1,0:T(8,128)S(1)}, f32[2,5,32,1024]{3,2,1,0:T(8,128)}, u32[]{:S(2)}, u32[]{:S(2)}) %collective-permute-start.3) | collective-permute-done | bytes 1310752 | tf_op jit(solution)/shard_map/ppermute | solution.py:19
  307.1 1.2 broadcast.4793
  308.3 53.7 %while.38 = (s32[]{:T(128)}, f32[2,5,32,1024]{3,2,1,0:T(8,128)}, f32[]{:T(128)}, f32[2,5,4,1024]{3,2,1,0:T(4,128)}, f32[2,5,32,1024]{3,2,1,0:T(8,128)S(1)}, /*in...) while((s32[]{:T(128)}, f32[2,5,32,1024]{3,2,1,0:T(8,128)}, ...), condition=%wide.region_15.18_spmd, body=%wide.region_11.17_spmd.sunk | while | flops 59260928 | bytes 91708440 | solution.py:240
  324.8 1.1 multiply_add_fusion.53
  326.5 1.3 constant_dynamic-update-slice_fusion.17
  330.5 1.4 multiply_add_fusion.52
  332.0 1.7 constant_dynamic-update-slice_fusion.16
  336.1 1.4 multiply_add_fusion.51
  337.5 1.6 constant_dynamic-update-slice_fusion.15
  340.0 1.3 fusion.388
  347.2 1.3 constant_dynamic-update-slice_fusion.17
  351.2 1.4 multiply_add_fusion.52
  352.7 1.7 constant_dynamic-update-slice_fusion.16
  356.8 1.4 multiply_add_fusion.51
  358.2 1.6 constant_dynamic-update-slice_fusion.15
  360.7 1.3 fusion.388
  362.0 3.1 add_multiply_fusion
  (357 shorter events, 75.7 us)
Async XLA Ops:
  0.0 74.1 %copy-start = (f32[2,5,32,1024]{3,2,1,0:T(8,128)S(1)}, f32[2,5,32,1024]{3,2,1,0:T(8,128)}, u32[]{:S(2)}) copy-start(f32[2,5,32,1024]{3,2,1,0:T(8,128)} %param.13) | copy-start | bytes 3932164
  0.0 16.8 %copy-start.8 = (s32[2,3]{1,0:T(2,128)S(1)}, s32[2,3]{1,0:T(2,128)}, u32[]{:S(2)}) copy-start(s32[2,3]{1,0:T(2,128)} %param.15) | copy-start | bytes 76
  1.9 72.1 %collective-permute-start = (f32[5,32,1024]{2,1,0:T(8,128)S(1)}, f32[5,32,1024]{2,1,0:T(8,128)S(1)}, u32[]{:S(2)}, u32[]{:S(2)}) collective-permute-start(f32[5,32,1024]{2,1,0:T(8,128)S(1)} %dynamic-slice_bitcast_fusion.16), channel_id=1, source_target_pairs={{0,256},{1,257},{2,258},{3,259},{4,260},{5,261},{6,262},{7,263},{8... | collective-permute-start | bytes 1966088 | tf_op jit(solution)/shard_map/ppermute | solution.py:23
  74.1 202.8 %copy-start.1 = (f32[5,32,1024]{2,1,0:T(8,128)}, f32[5,32,1024]{2,1,0:T(8,128)S(1)}, u32[]{:S(2)}) copy-start(f32[5,32,1024]{2,1,0:T(8,128)S(1)} %collective-permute-done) | copy-start | bytes 1966084
  75.4 130.4 %collective-permute-start.2 = (f32[2,5,32,1024]{3,2,1,0:T(8,128)}, f32[2,5,32,1024]{3,2,1,0:T(8,128)}, u32[]{:S(2)}, u32[]{:S(2)}) collective-permute-start(f32[2,5,32,1024]{3,2,1,0:T(8,128)} %broadcast_select_fusion), channel_id=1, source_target_pairs={{1,0},{2,1},{3,2},{4,3},{5,4},{6,5},{7,6},{8,7},{9,8},{10,9},{11,1... | collective-permute-start | bytes 3932168 | tf_op jit(solution)/shard_map/ppermute | solution.py:19
  77.3 130.1 %collective-permute-start.1 = (f32[2,5,32,1024]{3,2,1,0:T(8,128)}, f32[2,5,32,1024]{3,2,1,0:T(8,128)}, u32[]{:S(2)}, u32[]{:S(2)}) collective-permute-start(f32[2,5,32,1024]{3,2,1,0:T(8,128)} %broadcast_select_fusion), channel_id=1, source_target_pairs={{0,1},{1,2},{2,3},{3,4},{4,5},{5,6},{6,7},{7,8},{8,9},{9,10},{10,1... | collective-permute-start | bytes 3932168 | tf_op jit(solution)/shard_map/ppermute | solution.py:19
  247.6 1.3 copy-start.2
  249.4 1.1 copy-start.3
  274.0 1.3 copy-start.2
  275.8 1.1 copy-start.3
  278.5 17.2 %collective-permute-start.4 = (f32[2,5,32,1024]{3,2,1,0:T(8,128)S(1)}, f32[2,5,32,1024]{3,2,1,0:T(8,128)}, u32[]{:S(2)}, u32[]{:S(2)}) collective-permute-start(f32[2,5,32,1024]{3,2,1,0:T(8,128)S(1)} %fusion.308), channel_id=1, source_target_pairs={{1,0},{2,1},{3,2},{4,3},{5,4},{6,5},{7,6},{8,7},{9,8},{10,9},{11,1... | collective-permute-start | bytes 3932168 | tf_op jit(solution)/shard_map/ppermute | solution.py:19
  280.6 23.3 %collective-permute-start.3 = (f32[2,5,32,1024]{3,2,1,0:T(8,128)S(1)}, f32[2,5,32,1024]{3,2,1,0:T(8,128)}, u32[]{:S(2)}, u32[]{:S(2)}) collective-permute-start(f32[2,5,32,1024]{3,2,1,0:T(8,128)S(1)} %fusion.308), channel_id=1, source_target_pairs={{0,1},{1,2},{2,3},{3,4},{4,5},{5,6},{6,7},{7,8},{8,9},{9,10},{10,1... | collective-permute-start | bytes 3932168 | tf_op jit(solution)/shard_map/ppermute | solution.py:19
  328.5 0.9 copy-start.4
  328.5 1.0 copy-start.5
  333.7 0.9 copy-start.6
  333.7 1.0 copy-start.7
  349.2 0.9 copy-start.4
  349.2 1.0 copy-start.5
  354.4 0.9 copy-start.6
  354.5 1.0 copy-start.7
where the time goes:
time: 369 us; the launch traced here: 365 us
  blocking collectives  112 us (30%)
  other arithmetic  87.7 us (24%)
  waiting for transfers between devices  74 us (20%)
  local copies, waits for them, and re-layouts  40 us (11%)
  loops' own time  26.6 us (7%)
  starting transfers between devices  23.5 us (6%)
    pmax x1, blocking collectives, body(): ratio = COURANT / lax.pmax(local_fast, 'box')  112 us
    ppermute x1, waiting for transfers between devices, from_partner(): lax.ppermute(shard, axis, [(i, i ^ 1 << distance) for i in range(lax.axis...  56.8 us
    another operation x2, loops' own time, local_rate(): return lax.map(unpack_rate, (box_data, low_x, high_x, low_y, high_y))  26.6 us
    while x48, other arithmetic  20.1 us
    ppermute x4, waiting for transfers between devices, from_behind(): lax.ppermute(value, axis, [(source, source + steps) for source in range(i...  17.2 us
    ppermute x1, starting transfers between devices, from_partner(): lax.ppermute(shard, axis, [(i, i ^ 1 << distance) for i in range(lax.axis...  14.8 us
    add x8, other arithmetic, face_states(): upper_val = centre + flatten * up_part  11.3 us
    ppermute x4, starting transfers between devices, from_behind(): lax.ppermute(value, axis, [(source, source + steps) for source in range(i...  8.65 us
  transfers between devices with their start and end apart: 5, of which 3 were waited for; matrix products, arithmetic and copies ran while one was open for 5% of the time, Pallas kernels for 0%

commit v1 on v0

v1 whole, which is shorter than its diff:
```python
import functools

import jax
import jax.numpy as jnp
from jax import lax
from jax.experimental import pallas as pl
from jax.experimental.pallas import tpu as pltpu
from jax.sharding import PartitionSpec as P

BZC = 32
GHOST = 4
RIEMANN_ITERS = 3
COURANT = 0.4

XC = 32
TILES = 8
COLS = 16
PAD = 48
F32 = jnp.float32


def rcp(value):
    guess = pl.reciprocal(value, approx=True)
    return guess * (2.0 - value * guess)


def prims_of(cons):
    dens = jnp.maximum(cons[0], 0.05)
    inv = rcp(dens)
    v1, v2, v3 = cons[1] * inv, cons[2] * inv, cons[3] * inv
    internal = jnp.maximum(cons[4] * inv - 0.5 * (v1 * v1 + v2 * v2 + v3 * v3), 0.05)
    pres = dens * (0.4 * internal + 0.1 * dens)
    return dens, v1, v2, v3, pres


def face_parts(qm1, q0, q1, q2):
    diff = q1 - q0
    step = 0.5 * diff - (1.0 / 12.0) * ((q2 + qm1) - (q0 + q1))
    step = jnp.minimum(jnp.maximum(step, jnp.minimum(diff, 0.0)), jnp.maximum(diff, 0.0))
    return step, diff - step


def shock_of(pm2, pm1, p1, p2, vm1, v1):
    steep = jnp.abs(p1 - pm1) * rcp(jnp.abs(p2 - pm2) + 0.1 * (p2 + pm2))
    squeeze = jnp.maximum(vm1 - v1, 0.0)
    level = jnp.minimum(jnp.maximum(4.0 * steep - 3.0, 0.0), 1.0)
    return level * squeeze * rcp(squeeze + 0.2)


def minmod(first, second):
    return jnp.maximum(
        jnp.minimum(first, jnp.maximum(second, 0.0)), jnp.minimum(second, 0.0)
    )


def edge_states(centre, below, above, flatten):
    down = minmod(below, above + above)
    up = minmod(above, below + below)
    return centre - flatten * down, centre + flatten * up


def wave_side(dens, pres):
    cube = (0.05 * dens) * (dens * dens)
    both = dens * pres
    base = cube + 0.2 * both
    slope = 1.2 * dens + cube * rcp(pres)
    return base, slope, base + slope * pres


def riemann(left, right, normal):
    dens_l, pres_l, vel_l = left[0], left[4], left[normal]
    dens_r, pres_r, vel_r = right[0], right[4], right[normal]
    base_l, slope_l, imp_l = wave_side(dens_l, pres_l)
    base_r, slope_r, imp_r = wave_side(dens_r, pres_r)
    floor_p = 0.1 * jnp.minimum(pres_l, pres_r)
    gap = vel_r - vel_l
    inv_l, inv_r = lax.rsqrt(imp_l), lax.rsqrt(imp_r)
    guess = (pres_l * inv_l + pres_r * inv_r - gap) * rcp(inv_l + inv_r)
    guess = jnp.maximum(guess, floor_p)
    for _ in range(RIEMANN_ITERS):
        inv_l = lax.rsqrt(base_l + slope_l * guess)
        inv_r = lax.rsqrt(base_r + slope_r * guess)
        miss = gap + (guess - pres_l) * inv_l + (guess - pres_r) * inv_r
        weight = (inv_l + inv_l * (imp_l * (inv_l * inv_l))) + (
            inv_r + inv_r * (imp_r * (inv_r * inv_r))
        )
        guess = jnp.maximum(guess - (miss + miss) * rcp(weight), floor_p)
    inv_l = lax.rsqrt(base_l + slope_l * guess)
    inv_r = lax.rsqrt(base_r + slope_r * guess)
    star_l = vel_l - (guess - pres_l) * inv_l
    star_r = vel_r + (guess - pres_r) * inv_r
    speed = (star_l * inv_r + star_r * inv_l) * rcp(inv_l + inv_r)
    upwind = speed >= 0.0
    dens = jnp.where(upwind, dens_l, dens_r)
    pres = jnp.where(upwind, pres_l, pres_r)
    inv = jnp.where(upwind, inv_l, inv_r)
    inv_dens = rcp(dens)
    internal = jnp.maximum(2.5 * (pres * inv_dens - 0.1 * dens), 0.05)
    shrink = (guess - pres) * (inv * inv)
    star = rcp(inv_dens - shrink)
    internal = jnp.maximum(internal + 0.5 * (guess + pres) * shrink, 0.1 * internal)
    mass = star * speed
    kinetic = speed * speed
    momenta = []
    for component in range(1, 4):
        if component == normal:
            momenta.append(mass * speed + guess)
        else:
            carried = jnp.where(upwind, left[component], right[component])
            kinetic = kinetic + carried * carried
            momenta.append(mass * carried)
    energy = mass * (internal + 0.5 * kinetic) + speed * guess
    return [mass] + momenta + [energy]


def fastest_kernel(state_ref, out_ref):
    def step(index, best):
        box, tile = index // TILES, index % TILES
        lanes = pl.ds(pl.multiple_of(tile * 128, 128), 128)
        dens, v1, v2, v3, pres = prims_of([state_ref[box, f, :, lanes] for f in range(5)])
        square = (0.1 * dens * dens + 1.4 * pres) * rcp(dens)
        speed = jnp.abs(v1) + jnp.abs(v2) + jnp.abs(v3) + 3.0 * (square * lax.rsqrt(square))
        return jnp.maximum(best, speed)

    best = lax.fori_loop(0, COLS, step, jnp.zeros((XC, 128), F32))
    best = jnp.maximum(jnp.maximum(best[:8], best[8:16]), jnp.maximum(best[16:24], best[24:]))
    out_ref[...] = best


def plane_kernel(rows, state_ref, out_ref, prim, near, far, shock, low, high, flux):
    shape = (rows, 128)
    lane = lax.broadcasted_iota(jnp.int32, shape, 1)
    depth = lane % BZC

    def y_ahead(get, tile, steps):
        nxt = lax.rem(tile + 1, COLS)
        return pltpu.roll(
            jnp.where(lane < 32 * steps, get(nxt), get(tile)), 128 - 32 * steps, 1
        )

    def y_back(get, tile, steps):
        prv = lax.rem(tile + COLS - 1, COLS)
        return pltpu.roll(jnp.where(lane >= 128 - 32 * steps, get(prv), get(tile)), 32 * steps, 1)

    def z_ahead(value, steps):
        return jnp.where(
            depth < BZC - steps,
            pltpu.roll(value, 128 - steps, 1),
            pltpu.roll(value, BZC - steps, 1),
        )

    def z_back(value, steps):
        return jnp.where(
            depth >= steps, pltpu.roll(value, steps, 1), pltpu.roll(value, 128 + steps - BZC, 1)
        )

    def fill(tile, _):
        box, part = tile // TILES, tile % TILES
        lanes = pl.ds(pl.multiple_of(part * 128, 128), 128)
        values = prims_of([state_ref[box, f, :, lanes] for f in range(5)])
        for f in range(5):
            prim[f, tile] = values[f]
        return 0

    lax.fori_loop(0, COLS, fill, 0)

    def y_faces(tile, _):
        for f in range(5):
            get = lambda t, f=f: prim[f, t]
            here = get(tile)
            behind = y_back(get, tile, 1)
            ahead = y_ahead(get, tile, 1)
            second = y_ahead(get, tile, 2)
            near[f, tile], far[f, tile] = face_parts(behind, here, ahead, second)
            if f == 2:
                vel_m, vel_p = behind, ahead
            if f == 4:
                shock[tile] = shock_of(
                    y_back(get, tile, 2), behind, ahead, second, vel_m, vel_p
                )
        return 0

    lax.fori_loop(0, COLS, y_faces, 0)

    def y_states(tile, _):
        get = lambda t: shock[t]
        flatten = 1.0 - jnp.maximum(
            jnp.maximum(y_back(get, tile, 1), shock[tile]), y_ahead(get, tile, 1)
        )
        for f in range(5):
            below = y_back(lambda t, f=f: far[f, t], tile, 1)
            low[f, tile], high[f, tile] = edge_states(prim[f, tile], below, near[f, tile], flatten)
        return 0

    lax.fori_loop(0, COLS, y_states, 0)

    def y_flux(tile, _):
        left = [high[f, tile] for f in range(5)]
        right = [y_ahead(lambda t, f=f: low[f, t], tile, 1) for f in range(5)]
        values = riemann(left, right, 2)
        for f in range(5):
            flux[f, tile] = values[f]
        return 0

    lax.fori_loop(0, COLS, y_flux, 0)

    def z_sweep(tile, _):
        box, part = tile // TILES, tile % TILES
        lanes = pl.ds(pl.multiple_of(part * 128, 128), 128)
        parts = []
        for f in range(5):
            here = prim[f, tile]
            behind, ahead, second = z_back(here, 1), z_ahead(here, 1), z_ahead(here, 2)
            parts.append((here,) + face_parts(behind, here, ahead, second))
            if f == 3:
                vel_m, vel_p = behind, ahead
            if f == 4:
                level = shock_of(z_back(here, 2), behind, ahead, second, vel_m, vel_p)
        flatten = 1.0 - jnp.maximum(jnp.maximum(z_back(level, 1), level), z_ahead(level, 1))
        left, right = [], []
        for here, above, rest in parts:
            lower, upper = edge_states(here, z_back(rest, 1), above, flatten)
            left.append(upper)
            right.append(z_ahead(lower, 1))
        values = riemann(left, right, 3)
        for f in range(5):
            across = values[f] - z_back(values[f], 1)
            along = flux[f, tile] - y_back(lambda t, f=f: flux[f, t], tile, 1)
            out_ref[box, f, :, lanes] = across + along
        return 0

    lax.fori_loop(0, COLS, z_sweep, 0)


def line_kernel(
    stage, slot_ref, ratio_ref, state_ref, below_ref, above_ref, plane_ref, *rest
):
    if stage == 2:
        base_ref, out_ref, prim, near, far, shock, low, high, flux, end_low, end_high, end_flux = rest
    else:
        out_ref, prim, near, far, shock, low, high, flux, end_low, end_high, end_flux = rest

    def faces(tile, _):
        box, part = tile // TILES, tile % TILES
        lanes = pl.ds(pl.multiple_of(part * 128, 128), 128)
        start = tile * PAD
        inner = [state_ref[box, f, :, lanes] for f in range(5)]
        below_slot, above_slot = slot_ref[box, 0], slot_ref[box, 1]
        no_below, no_above = slot_ref[box, 2] != 0, slot_ref[box, 3] != 0
        under, over = [], []
        for f in range(5):
            first = jnp.broadcast_to(state_ref[box, f, 0:1, lanes], (GHOST, 128))
            last = jnp.broadcast_to(state_ref[box, f, XC - 1 : XC, lanes], (GHOST, 128))
            under.append(jnp.where(no_below, first, below_ref[below_slot, f, :, lanes]))
            over.append(jnp.where(no_above, last, above_ref[above_slot, f, :, lanes]))
        inner, under, over = prims_of(inner), prims_of(under), prims_of(over)
        for f in range(5):
            prim[f, pl.ds(start, GHOST)] = under[f]
            prim[f, pl.ds(start + GHOST, XC)] = inner[f]
            prim[f, pl.ds(start + GHOST + XC, GHOST)] = over[f]
        for f in range(5):
            here = prim[f, pl.ds(start + 2, 40)]
            behind = prim[f, pl.ds(start + 1, 40)]
            ahead = prim[f, pl.ds(start + 3, 40)]
            second = prim[f, pl.ds(start + 4, 40)]
            near[f, pl.ds(start + 2, 40)], far[f, pl.ds(start + 2, 40)] = face_parts(
                behind, here, ahead, second
            )
            if f == 1:
                vel_m, vel_p = behind, ahead
            if f == 4:
                shock[pl.ds(start + 2, 40)] = shock_of(
                    prim[f, pl.ds(start, 40)], behind, ahead, second, vel_m, vel_p
                )
        flatten = 1.0 - jnp.maximum(
            jnp.maximum(shock[pl.ds(start + 2, 40)], shock[pl.ds(start + 3, 40)]),
            shock[pl.ds(start + 4, 40)],
        )
        for f in range(5):
            lower, upper = edge_states(
                prim[f, pl.ds(start + 3, 40)],
                far[f, pl.ds(start + 2, 40)],
                near[f, pl.ds(start + 3, 40)],
                flatten,
            )
            low[f, pl.ds(start + 3, 40)] = lower
            high[f, pl.ds(start + 3, 40)] = upper
            end_high[f, pl.ds(tile, 1)] = high[f, pl.ds(start + 35, 1)]
            end_low[f, pl.ds(tile, 1)] = low[f, pl.ds(start + 36, 1)]
        return 0

    lax.fori_loop(0, COLS, faces, 0)

    def solve(tile, _):
        start = tile * PAD
        left = [high[f, pl.ds(start + 3, XC)] for f in range(5)]
        right = [low[f, pl.ds(start + 4, XC)] for f in range(5)]
        values = riemann(left, right, 1)
        for f in range(5):
            flux[f, pl.ds(start + 3, XC)] = values[f]
        return 0

    lax.fori_loop(0, COLS, solve, 0)
    values = riemann([end_high[f] for f in range(5)], [end_low[f] for f in range(5)], 1)
    for f in range(5):
        end_flux[f] = values[f]
    ratio = ratio_ref[0]

    def update(tile, _):
        box, part = tile // TILES, tile % TILES
        lanes = pl.ds(pl.multiple_of(part * 128, 128), 128)
        start = tile * PAD
        for f in range(5):
            flux[f, pl.ds(start + 35, 1)] = end_flux[f, pl.ds(tile, 1)]
            across = flux[f, pl.ds(start + 4, XC)] - flux[f, pl.ds(start + 3, XC)]
            rate = ratio * (across + plane_ref[box, f, :, lanes])
            here = state_ref[box, f, :, lanes]
            if stage == 1:
                out_ref[box, f, :, lanes] = here - rate
            else:
                out_ref[box, f, :, lanes] = 0.5 * (base_ref[box, f, :, lanes] + (here - rate))
        return 0

    lax.fori_loop(0, COLS, update, 0)


VMEM = pl.BlockSpec(memory_space=pltpu.VMEM)
SMEM = pl.BlockSpec(memory_space=pltpu.SMEM)
LIMIT = 48 << 20


def params():
    return pltpu.CompilerParams(vmem_limit_bytes=LIMIT)


def fastest(state):
    return pl.pallas_call(
        fastest_kernel,
        out_shape=jax.ShapeDtypeStruct((8, 128), F32),
        in_specs=[VMEM],
        out_specs=VMEM,
        compiler_params=params(),
        name="fastest",
    )(state)


def plane_sweeps(state):
    rows = state.shape[2]
    five = pltpu.VMEM((5, COLS, rows, 128), F32)
    one = pltpu.VMEM((COLS, rows, 128), F32)
    return pl.pallas_call(
        functools.partial(plane_kernel, rows),
        out_shape=jax.ShapeDtypeStruct(state.shape, F32),
        in_specs=[VMEM],
        out_specs=VMEM,
        scratch_shapes=[five, five, five, one, five, five, five],
        compiler_params=params(),
        cost_estimate=pl.CostEstimate(
            flops=60_000_000, bytes_accessed=2_700_000, transcendentals=0
        ),
        name="plane",
    )(state)


def line_sweep(stage, slots, ratio, state, below, above, plane, base=None):
    five = pltpu.VMEM((5, COLS * PAD, 128), F32)
    one = pltpu.VMEM((COLS * PAD, 128), F32)
    end = pltpu.VMEM((5, COLS, 128), F32)
    args = [slots, ratio, state, below, above, plane]
    if stage == 2:
        args.append(base)
    return pl.pallas_call(
        functools.partial(line_kernel, stage),
        out_shape=jax.ShapeDtypeStruct(state.shape, F32),
        in_specs=[SMEM, SMEM] + [VMEM] * (len(args) - 2),
        out_specs=VMEM,
        scratch_shapes=[five, five, five, one, five, five, five, end, end, end],
        compiler_params=params(),
        cost_estimate=pl.CostEstimate(
            flops=30_000_000, bytes_accessed=4_000_000, transcendentals=0
        ),
        name="line",
    )(*args)


def shifted(value, steps):
    count = lax.axis_size("box")
    first, last = max(0, -steps), min(count, count - steps)
    return lax.ppermute(value, "box", [(s, s + steps) for s in range(first, last)])


def all_max(value):
    count = lax.axis_size("box")
    inner = min(count, 32)
    outer = count // inner
    along = [[inner * k + i for k in range(outer)] for i in range(inner)]
    level = [[inner * k + i for i in range(inner)] for k in range(outer)]
    value = jnp.max(lax.all_gather(value, "box", axis_index_groups=level), axis=0)
    value = jnp.max(lax.all_gather(value, "box", axis_index_groups=along), axis=0)
    return jnp.max(value)


def body(cell_state, swap_slots, neighbours):
    slots = cell_state.shape[0]
    count = lax.axis_size("box")
    chosen_slot = swap_slots[0]
    outgoing = lax.dynamic_index_in_dim(cell_state, chosen_slot, 0, keepdims=False)
    incoming = lax.ppermute(outgoing, "box", [(i, i ^ (count // 2)) for i in range(count)])
    ratio = (COURANT / all_max(fastest(cell_state))).reshape(1)
    chosen = jnp.arange(slots, dtype=jnp.int32) == chosen_slot
    after = jnp.where(chosen[:, None, None, None], incoming[None], cell_state)
    own_start = lax.axis_index("box") * slots
    lower, upper = neighbours[:, 0], neighbours[:, 1]
    table = jnp.stack(
        [
            jnp.clip(lower - own_start + slots, 0, slots - 1),
            jnp.clip(upper - own_start - slots, 0, slots - 1),
            (lower < 0).astype(jnp.int32),
            (upper < 0).astype(jnp.int32),
        ],
        axis=1,
    )
    below = shifted(after[:, :, -GHOST:], 1)
    above = shifted(after[:, :, :GHOST], -1)
    first = line_sweep(1, table, ratio, after, below, above, plane_sweeps(after))
    below = shifted(first[:, :, -GHOST:], 1)
    above = shifted(first[:, :, :GHOST], -1)
    return line_sweep(2, table, ratio, first, below, above, plane_sweeps(first), after)


def solution(mesh):
    in_specs = (P("box", None, None, None), P("box"), P("box", None))
    out_specs = P("box", None, None, None)
    return jax.shard_map(body, mesh=mesh, in_specs=in_specs, out_specs=out_specs, check_vma=False)
```

time: 369 us -> 173 us (0.47)
  the two profiles are of different devices: /device:TPU:32 before, /device:TPU:1 now
where the time goes in v1:
time: 173 us
  blocking collectives  79.6 us (46%)
  Pallas kernels  51.4 us (30%)
  starting transfers between devices  38 us (22%)
    all_gather x1, blocking collectives, all_max(): lax.all_gather(value, 'box', axis_index_groups=along)  53.9 us
    pallas_call x2, Pallas kernels, plane_sweeps(): pl.pallas_call(functools.partial(plane_kernel, rows), out_shape=jax.Shape...  36.4 us
    all_gather x1, blocking collectives, all_max(): lax.all_gather(value, 'box', axis_index_groups=level)  25.7 us
    ppermute x4, starting transfers between devices, shifted(): lax.ppermute(value, 'box', [(s, s + steps) for s in range(first, last)])  21.7 us
    ppermute x1, starting transfers between devices, body(): lax.ppermute(outgoing, 'box', [(i, i ^ count // 2) for i in range(count)])  16.3 us
    pallas_call x2, Pallas kernels, line_sweep(): pl.pallas_call(functools.partial(line_kernel, stage), out_shape=jax.Shape...  14.3 us
  transfers between devices with their start and end apart: 5, of which 0 were waited for; matrix products, arithmetic and copies ran while one was open for 1% of the time, Pallas kernels for 21%

profile of v1, /device:TPU:1, one launch (start us, length us, event | category | flops | bytes accessed | tf_op | source)
XLA Modules:
  0.0 173.0 jit_solution(11909253597980637433)
XLA Ops:
  0.0 0.0 copy-start
  0.8 0.0 copy-start.1
  0.8 1.1 dynamic-slice_bitcast_fusion
  1.9 16.3 %collective-permute-start = (f32[5,32,1024]{2,1,0:T(8,128)S(1)}, f32[5,32,1024]{2,1,0:T(8,128)S(1)}, u32[]{:S(2)}, u32[]{:S(2)}) collective-permute-start(f32[5,32,1024]{2,1,0:T(8,128)S(1)} %dynamic-slice_bitcast_fusion), channel_id=1, source_target_pairs={{0,256},{1,257},{2,258},{3,259},{4,260},{5,261},{6,262},{7,263},{8... | collective-permute-start | bytes 1966088 | tf_op jit(solution)/shard_map/ppermute | solution.py:408
  18.2 0.0 copy-done
  18.2 0.7 fastest.1
  18.9 25.7 %all-gather = f32[256,128]{1,0:T(8,128)S(1)} all-gather(f32[8,128]{1,0:T(8,128)S(1)} %fastest.1), channel_id=2, replica_groups={{0,1,2,3,4,5,6,7,8,9,10,11,12,13,14,15,16,17,18,19,20,21,22,23,24,25,26..., dimensions={0}, use_global_device_ids=true | all-gather | bytes 135168 | tf_op jit(solution)/shard_map/all_gather | solution.py:398
  44.6 0.0 copy-done.1
  44.6 0.1 compare_convert_fusion.1
  44.7 0.1 add_clamp_fusion.1
  44.8 0.0 collective-permute-done
  44.8 0.3 broadcast_select_fusion.state_ref.rest_0_
  45.0 0.1 fusion.1
  45.1 2.1 %collective-permute-start.2 = (f32[2,5,4,1024]{3,2,1,0:T(4,128)S(1)}, f32[2,5,4,1024]{3,2,1,0:T(4,128)S(1)}, u32[]{:S(2)}, u32[]{:S(2)}) collective-permute-start(f32[2,5,4,1024]{3,2,1,0:T(4,128)S(1)} %get-tuple-element.7), channel_id=1, source_target_pairs={{1,0},{2,1},{3,2},{4,3},{5,4},{6,5},{7,6},{8,7},{9,8},{10,9},{11,1... | collective-permute-start | bytes 491528 | tf_op jit(solution)/shard_map/ppermute | solution.py:389
  47.2 3.5 %collective-permute-start.1 = (f32[2,5,4,1024]{3,2,1,0:T(4,128)S(1)}, f32[2,5,4,1024]{3,2,1,0:T(4,128)S(1)}, u32[]{:S(2)}, u32[]{:S(2)}) collective-permute-start(f32[2,5,4,1024]{3,2,1,0:T(4,128)S(1)} %get-tuple-element.8), channel_id=1, source_target_pairs={{0,1},{1,2},{2,3},{3,4},{4,5},{5,6},{6,7},{7,8},{8,9},{9,10},{10,1... | collective-permute-start | bytes 491528 | tf_op jit(solution)/shard_map/ppermute | solution.py:389
  50.7 53.9 %all-gather.1 = f32[128,128]{1,0:T(8,128)S(1)} all-gather(f32[8,128]{1,0:T(8,128)S(1)} %bitcast_reduce_fusion), channel_id=3, replica_groups={{0,32,64,96,128,160,192,224,256,288,320,352,384,416,448,480},{1,33,65,9..., dimensions={0}, use_global_device_ids=true | all-gather | bytes 69632 | tf_op jit(solution)/shard_map/all_gather | solution.py:399
  104.6 0.6 reduce_max.20
  105.9 0.1 pad_add_fusion.slot_ref
  106.0 18.2 %plane.2.plane_ref = f32[2,5,32,1024]{3,2,1,0:T(8,128)S(1)} custom-call(f32[2,5,32,1024]{3,2,1,0:T(8,128)S(1)} %broadcast_select_fusion.state_ref.rest_0_), custom_call_target="tpu_custom_call" | custom-call | flops 60000000 | bytes 2700000 | tf_op jit(solution)/shard_map/plane/pallas_call | solution.py:351
  124.2 0.0 collective-permute-done.2.above_ref
  124.2 0.0 collective-permute-done.1.below_ref
  124.2 6.5 %line.2.state_ref = f32[2,5,32,1024]{3,2,1,0:T(8,128)S(1)} custom-call(s32[2,4]{1,0:T(2,128)S(1)} %pad_add_fusion.slot_ref, f32[1]{0:T(128)} %bitcast.1.ratio_ref, f32[2,5,32,1024]{3,2,1,0:T(8,128)S(1)} %broadcast_select_fusion.state_ref.rest_0_, f32[2,5,4,1024]{3,2,1,0:T(4,128)S(1)} %collective-permute-done.1.below_ref, ...), custom_call_target="tpu_custom_call" | custom-call | flops 30000000 | bytes 4000000 | tf_op jit(solution)/shard_map/line/pallas_call | solution.py:372
  130.8 0.1 fusion
  130.8 14.2 %collective-permute-start.4 = (f32[2,5,4,1024]{3,2,1,0:T(4,128)S(1)}, f32[2,5,4,1024]{3,2,1,0:T(4,128)S(1)}, u32[]{:S(2)}, u32[]{:S(2)}) collective-permute-start(f32[2,5,4,1024]{3,2,1,0:T(4,128)S(1)} %get-tuple-element.5), channel_id=1, source_target_pairs={{1,0},{2,1},{3,2},{4,3},{5,4},{6,5},{7,6},{8,7},{9,8},{10,9},{11,1... | collective-permute-start | bytes 491528 | tf_op jit(solution)/shard_map/ppermute | solution.py:389
  145.0 1.9 %collective-permute-start.3 = (f32[2,5,4,1024]{3,2,1,0:T(4,128)S(1)}, f32[2,5,4,1024]{3,2,1,0:T(4,128)S(1)}, u32[]{:S(2)}, u32[]{:S(2)}) collective-permute-start(f32[2,5,4,1024]{3,2,1,0:T(4,128)S(1)} %get-tuple-element.6), channel_id=1, source_target_pairs={{0,1},{1,2},{2,3},{3,4},{4,5},{5,6},{6,7},{7,8},{8,9},{9,10},{10,1... | collective-permute-start | bytes 491528 | tf_op jit(solution)/shard_map/ppermute | solution.py:389
  147.0 18.2 %plane.3.plane_ref = f32[2,5,32,1024]{3,2,1,0:T(8,128)S(1)} custom-call(f32[2,5,32,1024]{3,2,1,0:T(8,128)S(1)} %line.2.state_ref), custom_call_target="tpu_custom_call" | custom-call | flops 60000000 | bytes 2700000 | tf_op jit(solution)/shard_map/plane/pallas_call | solution.py:351
  165.2 0.0 collective-permute-done.4.above_ref
  165.2 0.0 collective-permute-done.3.below_ref
  165.2 7.8 %line.3 = f32[2,5,32,1024]{3,2,1,0:T(8,128)} custom-call(s32[2,4]{1,0:T(2,128)S(1)} %pad_add_fusion.slot_ref, f32[1]{0:T(128)} %bitcast.1.ratio_ref, f32[2,5,32,1024]{3,2,1,0:T(8,128)S(1)} %line.2.state_ref, f32[2,5,4,1024]{3,2,1,0:T(4,128)S(1)} %collective-permute-done.3.below_ref, f32[2,5,4,1024]{3,2,1,0:T(4,128)S(1)} %collective-permute-done.4.above_ref, ...), custom_call_target="tpu_custom_call" | custom-call | flops 30000000 | bytes 4000000 | tf_op jit(solution)/shard_map/line/pallas_call | solution.py:372
  (2 shorter events, 0.0 us)
Async XLA Ops:
  0.0 18.2 %copy-start = (f32[2,5,32,1024]{3,2,1,0:T(8,128)S(1)}, f32[2,5,32,1024]{3,2,1,0:T(8,128)}, u32[]{:S(2)}) copy-start(f32[2,5,32,1024]{3,2,1,0:T(8,128)} %state_ref.1) | copy-start | bytes 3932164
  0.8 43.9 %copy-start.1 = (s32[2,3]{1,0:T(2,128)S(1)}, s32[2,3]{1,0:T(2,128)}, u32[]{:S(2)}) copy-start(s32[2,3]{1,0:T(2,128)} %param.5) | copy-start | bytes 76
  1.9 42.9 %collective-permute-start = (f32[5,32,1024]{2,1,0:T(8,128)S(1)}, f32[5,32,1024]{2,1,0:T(8,128)S(1)}, u32[]{:S(2)}, u32[]{:S(2)}) collective-permute-start(f32[5,32,1024]{2,1,0:T(8,128)S(1)} %dynamic-slice_bitcast_fusion), channel_id=1, source_target_pairs={{0,256},{1,257},{2,258},{3,259},{4,260},{5,261},{6,262},{7,263},{8... | collective-permute-start | bytes 1966088 | tf_op jit(solution)/shard_map/ppermute | solution.py:408
  45.1 79.1 %collective-permute-start.2 = (f32[2,5,4,1024]{3,2,1,0:T(4,128)S(1)}, f32[2,5,4,1024]{3,2,1,0:T(4,128)S(1)}, u32[]{:S(2)}, u32[]{:S(2)}) collective-permute-start(f32[2,5,4,1024]{3,2,1,0:T(4,128)S(1)} %get-tuple-element.7), channel_id=1, source_target_pairs={{1,0},{2,1},{3,2},{4,3},{5,4},{6,5},{7,6},{8,7},{9,8},{10,9},{11,1... | collective-permute-start | bytes 491528 | tf_op jit(solution)/shard_map/ppermute | solution.py:389
  47.2 77.0 %collective-permute-start.1 = (f32[2,5,4,1024]{3,2,1,0:T(4,128)S(1)}, f32[2,5,4,1024]{3,2,1,0:T(4,128)S(1)}, u32[]{:S(2)}, u32[]{:S(2)}) collective-permute-start(f32[2,5,4,1024]{3,2,1,0:T(4,128)S(1)} %get-tuple-element.8), channel_id=1, source_target_pairs={{0,1},{1,2},{2,3},{3,4},{4,5},{5,6},{6,7},{7,8},{8,9},{9,10},{10,1... | collective-permute-start | bytes 491528 | tf_op jit(solution)/shard_map/ppermute | solution.py:389
  130.8 34.4 %collective-permute-start.4 = (f32[2,5,4,1024]{3,2,1,0:T(4,128)S(1)}, f32[2,5,4,1024]{3,2,1,0:T(4,128)S(1)}, u32[]{:S(2)}, u32[]{:S(2)}) collective-permute-start(f32[2,5,4,1024]{3,2,1,0:T(4,128)S(1)} %get-tuple-element.5), channel_id=1, source_target_pairs={{1,0},{2,1},{3,2},{4,3},{5,4},{6,5},{7,6},{8,7},{9,8},{10,9},{11,1... | collective-permute-start | bytes 491528 | tf_op jit(solution)/shard_map/ppermute | solution.py:389
  145.0 20.2 %collective-permute-start.3 = (f32[2,5,4,1024]{3,2,1,0:T(4,128)S(1)}, f32[2,5,4,1024]{3,2,1,0:T(4,128)S(1)}, u32[]{:S(2)}, u32[]{:S(2)}) collective-permute-start(f32[2,5,4,1024]{3,2,1,0:T(4,128)S(1)} %get-tuple-element.6), channel_id=1, source_target_pairs={{0,1},{1,2},{2,3},{3,4},{4,5},{5,6},{6,7},{7,8},{8,9},{9,10},{10,1... | collective-permute-start | bytes 491528 | tf_op jit(solution)/shard_map/ppermute | solution.py:389

commit v2 on v1

--- a/solution.py
+++ b/solution.py
@@ -15,6 +15,8 @@
 XC = 32
 TILES = 8
 COLS = 16
+QUARTER = XC // 4
+LEVEL = 32
 PAD = 48
 F32 = jnp.float32
 
@@ -127,10 +129,22 @@
     out_ref[...] = best
 
 
-def plane_kernel(rows, state_ref, out_ref, prim, near, far, shock, low, high, flux):
-    shape = (rows, 128)
-    lane = lax.broadcasted_iota(jnp.int32, shape, 1)
-    depth = lane % BZC
+def columns(step, group=1):
+    def turn(index, _):
+        for k in range(group):
+            step(index * group + k)
+        return 0
+
+    lax.fori_loop(0, COLS // group, turn, 0)
+
+
+def plane_kernel(
+    rows, state_ref, out_ref, prim, near, far, shock, low, high, flux,
+    zprim, znear, zfar, zshock, zlow, zhigh, zflux,
+):
+    lane = lax.broadcasted_iota(jnp.int32, (rows, 128), 1)
+    joined = 128 // rows
+    ratio = XC // rows
 
     def y_ahead(get, tile, steps):
         nxt = lax.rem(tile + 1, COLS)
@@ -142,29 +156,28 @@
         prv = lax.rem(tile + COLS - 1, COLS)
         return pltpu.roll(jnp.where(lane >= 128 - 32 * steps, get(prv), get(tile)), 32 * steps, 1)
 
-    def z_ahead(value, steps):
-        return jnp.where(
-            depth < BZC - steps,
-            pltpu.roll(value, 128 - steps, 1),
-            pltpu.roll(value, BZC - steps, 1),
-        )
-
-    def z_back(value, steps):
-        return jnp.where(
-            depth >= steps, pltpu.roll(value, steps, 1), pltpu.roll(value, 128 + steps - BZC, 1)
-        )
-
-    def fill(tile, _):
+    def fill(tile):
         box, part = tile // TILES, tile % TILES
         lanes = pl.ds(pl.multiple_of(part * 128, 128), 128)
         values = prims_of([state_ref[box, f, :, lanes] for f in range(5)])
         for f in range(5):
             prim[f, tile] = values[f]
+
+    columns(fill, ratio)
+
+    def turn_in(quad, _):
+        for f in range(5):
+            turned = prim[f, pl.ds(quad * joined, joined)].reshape(128, 128).T
+            for k in range(4):
+                start = (quad * 4 + k) * PAD
+                zprim[f, pl.ds(start + 8, BZC)] = turned[BZC * k : BZC * (k + 1)]
+                zprim[f, pl.ds(start + 6, 2)] = zprim[f, pl.ds(start + 38, 2)]
+                zprim[f, pl.ds(start + 40, 2)] = zprim[f, pl.ds(start + 8, 2)]
         return 0
 
-    lax.fori_loop(0, COLS, fill, 0)
-
-    def y_faces(tile, _):
+    lax.fori_loop(0, COLS // joined, turn_in, 0)
+
+    def y_faces(tile):
         for f in range(5):
             get = lambda t, f=f: prim[f, t]
             here = get(tile)
@@ -178,11 +191,40 @@
                 shock[tile] = shock_of(
                     y_back(get, tile, 2), behind, ahead, second, vel_m, vel_p
                 )
-        return 0
-
-    lax.fori_loop(0, COLS, y_faces, 0)
-
-    def y_states(tile, _):
+
+    def z_faces(tile):
+        start = tile * PAD
+        for f in range(5):
+            here = zprim[f, pl.ds(start + 8, BZC)]
+            behind = zprim[f, pl.ds(start + 7, BZC)]
+            ahead = zprim[f, pl.ds(start + 9, BZC)]
+            second = zprim[f, pl.ds(start + 10, BZC)]
+            rise, rest = face_parts(behind, here, ahead, second)
+            znear[f, pl.ds(start + 8, BZC)] = rise
+            zfar[f, pl.ds(start + 8, BZC)] = rest
+            zfar[f, pl.ds(start + 7, 1)] = rest[BZC - 1 :]
+            if f == 3:
+                vel_m, vel_p = behind, ahead
+            if f == 4:
+                level = shock_of(
+                    zprim[f, pl.ds(start + 6, BZC)], behind, ahead, second, vel_m, vel_p
+                )
+                zshock[pl.ds(start + 8, BZC)] = level
+                zshock[pl.ds(start + 7, 1)] = level[BZC - 1 :]
+                zshock[pl.ds(start + 40, 1)] = level[:1]
+
+    def both(y_step, z_step):
+        def turn(index, _):
+            for k in range(ratio):
+                y_step(index * ratio + k)
+            z_step(index)
+            return 0
+
+        lax.fori_loop(0, COLS // ratio, turn, 0)
+
+    both(y_faces, z_faces)
+
+    def y_states(tile):
         get = lambda t: shock[t]
         flatten = 1.0 - jnp.maximum(
             jnp.maximum(y_back(get, tile, 1), shock[tile]), y_ahead(get, tile, 1)
@@ -190,67 +232,96 @@
         for f in range(5):
             below = y_back(lambda t, f=f: far[f, t], tile, 1)
             low[f, tile], high[f, tile] = edge_states(prim[f, tile], below, near[f, tile], flatten)
-        return 0
-
-    lax.fori_loop(0, COLS, y_states, 0)
-
-    def y_flux(tile, _):
+
+    def z_states(tile):
+        start = tile * PAD
+        flatten = 1.0 - jnp.maximum(
+            jnp.maximum(zshock[pl.ds(start + 7, BZC)], zshock[pl.ds(start + 8, BZC)]),
+            zshock[pl.ds(start + 9, BZC)],
+        )
+        for f in range(5):
+            lower, upper = edge_states(
+                zprim[f, pl.ds(start + 8, BZC)],
+                zfar[f, pl.ds(start + 7, BZC)],
+                znear[f, pl.ds(start + 8, BZC)],
+                flatten,
+            )
+            zlow[f, pl.ds(start + 8, BZC)] = lower
+            zlow[f, pl.ds(start + 40, 1)] = lower[:1]
+            zhigh[f, pl.ds(start + 8, BZC)] = upper
+
+    both(y_states, z_states)
+
+    def y_flux(tile):
         left = [high[f, tile] for f in range(5)]
         right = [y_ahead(lambda t, f=f: low[f, t], tile, 1) for f in range(5)]
         values = riemann(left, right, 2)
         for f in range(5):
             flux[f, tile] = values[f]
+
+    def z_flux(tile):
+        start = tile * PAD
+        left = [zhigh[f, pl.ds(start + 8, BZC)] for f in range(5)]
+        right = [zlow[f, pl.ds(start + 9, BZC)] for f in range(5)]
+        values = riemann(left, right, 3)
+        for f in range(5):
+            zflux[f, pl.ds(start + 8, BZC)] = values[f]
+            zflux[f, pl.ds(start + 7, 1)] = values[f][BZC - 1 :]
+
+    both(y_flux, z_flux)
+
+    def turn_out(quad, _):
+        for f in range(5):
+            across = []
+            for k in range(4):
+                start = (quad * 4 + k) * PAD
+                across.append(zflux[f, pl.ds(start + 8, BZC)] - zflux[f, pl.ds(start + 7, BZC)])
+            turned = jnp.concatenate(across, axis=0).T
+            for k in range(joined):
+                tile = quad * joined + k
+                box, part = tile // TILES, tile % TILES
+                lanes = pl.ds(pl.multiple_of(part * 128, 128), 128)
+                along = flux[f, tile] - y_back(lambda t, f=f: flux[f, t], tile, 1)
+                out_ref[box, f, :, lanes] = along + turned[rows * k : rows * (k + 1)]
         return 0
 
-    lax.fori_loop(0, COLS, y_flux, 0)
-
-    def z_sweep(tile, _):
-        box, part = tile // TILES, tile % TILES
-        lanes = pl.ds(pl.multiple_of(part * 128, 128), 128)
-        parts = []
-        for f in range(5):
-            here = prim[f, tile]
-            behind, ahead, second = z_back(here, 1), z_ahead(here, 1), z_ahead(here, 2)
-            parts.append((here,) + face_parts(behind, here, ahead, second))
-            if f == 3:
-                vel_m, vel_p = behind, ahead
-            if f == 4:
-                level = shock_of(z_back(here, 2), behind, ahead, second, vel_m, vel_p)
-        flatten = 1.0 - jnp.maximum(jnp.maximum(z_back(level, 1), level), z_ahead(level, 1))
-        left, right = [], []
-        for here, above, rest in parts:
-            lower, upper = edge_states(here, z_back(rest, 1), above, flatten)
-            left.append(upper)
-            right.append(z_ahead(lower, 1))
-        values = riemann(left, right, 3)
-        for f in range(5):
-            across = values[f] - z_back(values[f], 1)
-            along = flux[f, tile] - y_back(lambda t, f=f: flux[f, t], tile, 1)
-            out_ref[box, f, :, lanes] = across + along
-        return 0
-
-    lax.fori_loop(0, COLS, z_sweep, 0)
-
-
-def line_kernel(
-    stage, slot_ref, ratio_ref, state_ref, below_ref, above_ref, plane_ref, *rest
-):
-    if stage == 2:
-        base_ref, out_ref, prim, near, far, shock, low, high, flux, end_low, end_high, end_flux = rest
-    else:
-        out_ref, prim, near, far, shock, low, high, flux, end_low, end_high, end_flux = rest
-
-    def faces(tile, _):
+    lax.fori_loop(0, COLS // joined, turn_out, 0)
+
+
+def whole(refs, box, field, lanes):
+    if len(refs) == 1:
+        return refs[0][box, field, :, lanes]
+    outer, second, third = refs
+    return jnp.concatenate(
+        [
+            outer[box, field, :QUARTER, lanes],
+            second[box, field, :, lanes],
+            third[box, field, :, lanes],
+            outer[box, field, QUARTER:, lanes],
+        ],
+        axis=0,
+    )
+
+
+def line_kernel(counts, slot_ref, ratio_ref, below_ref, above_ref, *refs):
+    groups = []
+    for n in counts:
+        groups.append(refs[:n])
+        refs = refs[n:]
+    state, plane, base = groups
+    out_ref, prim, near, far, shock, low, high, flux, end_low, end_high, end_flux = refs
+
+    def faces(tile):
         box, part = tile // TILES, tile % TILES
         lanes = pl.ds(pl.multiple_of(part * 128, 128), 128)
         start = tile * PAD
-        inner = [state_ref[box, f, :, lanes] for f in range(5)]
+        inner = [whole(state, box, f, lanes) for f in range(5)]
         below_slot, above_slot = slot_ref[box, 0], slot_ref[box, 1]
         no_below, no_above = slot_ref[box, 2] != 0, slot_ref[box, 3] != 0
         under, over = [], []
         for f in range(5):
-            first = jnp.broadcast_to(state_ref[box, f, 0:1, lanes], (GHOST, 128))
-            last = jnp.broadcast_to(state_ref[box, f, XC - 1 : XC, lanes], (GHOST, 128))
+            first = jnp.broadcast_to(inner[f][:1], (GHOST, 128))
+            last = jnp.broadcast_to(inner[f][XC - 1 :], (GHOST, 128))
             under.append(jnp.where(no_below, first, below_ref[below_slot, f, :, lanes]))
             over.append(jnp.where(no_above, last, above_ref[above_slot, f, :, lanes]))
         inner, under, over = prims_of(inner), prims_of(under), prims_of(over)
@@ -287,41 +358,36 @@
             high[f, pl.ds(start + 3, 40)] = upper
             end_high[f, pl.ds(tile, 1)] = high[f, pl.ds(start + 35, 1)]
             end_low[f, pl.ds(tile, 1)] = low[f, pl.ds(start + 36, 1)]
-        return 0
-
-    lax.fori_loop(0, COLS, faces, 0)
-
-    def solve(tile, _):
+
+    columns(faces)
+
+    def solve(tile):
         start = tile * PAD
         left = [high[f, pl.ds(start + 3, XC)] for f in range(5)]
         right = [low[f, pl.ds(start + 4, XC)] for f in range(5)]
         values = riemann(left, right, 1)
         for f in range(5):
             flux[f, pl.ds(start + 3, XC)] = values[f]
-        return 0
-
-    lax.fori_loop(0, COLS, solve, 0)
+
+    columns(solve, 2)
     values = riemann([end_high[f] for f in range(5)], [end_low[f] for f in range(5)], 1)
     for f in range(5):
         end_flux[f] = values[f]
     ratio = ratio_ref[0]
 
-    def update(tile, _):
+    def update(tile):
         box, part = tile // TILES, tile % TILES
         lanes = pl.ds(pl.multiple_of(part * 128, 128), 128)
         start = tile * PAD
         for f in range(5):
             flux[f, pl.ds(start + 35, 1)] = end_flux[f, pl.ds(tile, 1)]
             across = flux[f, pl.ds(start + 4, XC)] - flux[f, pl.ds(start + 3, XC)]
-            rate = ratio * (across + plane_ref[box, f, :, lanes])
-            here = state_ref[box, f, :, lanes]
-            if stage == 1:
-                out_ref[box, f, :, lanes] = here - rate
-            else:
-                out_ref[box, f, :, lanes] = 0.5 * (base_ref[box, f, :, lanes] + (here - rate))
-        return 0
-
-    lax.fori_loop(0, COLS, update, 0)
+            value = whole(state, box, f, lanes) - ratio * (across + whole(plane, box, f, lanes))
+            if base:
+                value = 0.5 * (whole(base, box, f, lanes) + value)
+            out_ref[box, f, :, lanes] = value
+
+    columns(update)
 
 
 VMEM = pl.BlockSpec(memory_space=pltpu.VMEM)
@@ -346,32 +412,35 @@
 
 def plane_sweeps(state):
     rows = state.shape[2]
+    depth = COLS * rows // XC * PAD
     five = pltpu.VMEM((5, COLS, rows, 128), F32)
     one = pltpu.VMEM((COLS, rows, 128), F32)
+    five_z = pltpu.VMEM((5, depth, 128), F32)
+    one_z = pltpu.VMEM((depth, 128), F32)
     return pl.pallas_call(
         functools.partial(plane_kernel, rows),
         out_shape=jax.ShapeDtypeStruct(state.shape, F32),
         in_specs=[VMEM],
         out_specs=VMEM,
-        scratch_shapes=[five, five, five, one, five, five, five],
+        scratch_shapes=[five, five, five, one, five, five, five]
+        + [five_z, five_z, five_z, one_z, five_z, five_z, five_z],
         compiler_params=params(),
         cost_estimate=pl.CostEstimate(
-            flops=60_000_000, bytes_accessed=2_700_000, transcendentals=0
+            flops=2_000_000 * rows, bytes_accessed=90_000 * rows, transcendentals=0
         ),
         name="plane",
     )(state)
 
 
-def line_sweep(stage, slots, ratio, state, below, above, plane, base=None):
+def line_sweep(slots, ratio, below, above, state, plane, base=()):
     five = pltpu.VMEM((5, COLS * PAD, 128), F32)
     one = pltpu.VMEM((COLS * PAD, 128), F32)
     end = pltpu.VMEM((5, COLS, 128), F32)
-    args = [slots, ratio, state, below, above, plane]
-    if stage == 2:
-        args.append(base)
+    args = [slots, ratio, below, above, *state, *plane, *base]
+    shape = (slots.shape[0], 5, XC, TILES * 128)
     return pl.pallas_call(
-        functools.partial(line_kernel, stage),
-        out_shape=jax.ShapeDtypeStruct(state.shape, F32),
+        functools.partial(line_kernel, (len(state), len(plane), len(base))),
+        out_shape=jax.ShapeDtypeStruct(shape, F32),
         in_specs=[SMEM, SMEM] + [VMEM] * (len(args) - 2),
         out_specs=VMEM,
         scratch_shapes=[five, five, five, one, five, five, five, end, end, end],
@@ -389,26 +458,46 @@
     return lax.ppermute(value, "box", [(s, s + steps) for s in range(first, last)])
 
 
-def all_max(value):
+def level_max(value):
     count = lax.axis_size("box")
-    inner = min(count, 32)
-    outer = count // inner
-    along = [[inner * k + i for k in range(outer)] for i in range(inner)]
-    level = [[inner * k + i for i in range(inner)] for k in range(outer)]
-    value = jnp.max(lax.all_gather(value, "box", axis_index_groups=level), axis=0)
-    value = jnp.max(lax.all_gather(value, "box", axis_index_groups=along), axis=0)
-    return jnp.max(value)
+    inner = min(count, LEVEL)
+    level = [[inner * k + i for i in range(inner)] for k in range(count // inner)]
+    return jnp.max(lax.all_gather(value, "box", axis_index_groups=level), axis=0)
+
+
+def turned(value, levels):
+    count = lax.axis_size("box")
+    return lax.ppermute(value, "box", [(i, (i + levels * LEVEL) % count) for i in range(count)])
+
+
+def quarters(value, *wanted):
+    parts = [value[..., QUARTER * k : QUARTER * (k + 1), :] for k in wanted]
+    return jnp.concatenate(parts, axis=-2) if len(parts) > 1 else parts[0]
 
 
 def body(cell_state, swap_slots, neighbours):
     slots = cell_state.shape[0]
     count = lax.axis_size("box")
     chosen_slot = swap_slots[0]
+    chosen = (jnp.arange(slots, dtype=jnp.int32) == chosen_slot)[:, None, None, None]
+    levels = max(1, count // LEVEL)
     outgoing = lax.dynamic_index_in_dim(cell_state, chosen_slot, 0, keepdims=False)
-    incoming = lax.ppermute(outgoing, "box", [(i, i ^ (count // 2)) for i in range(count)])
-    ratio = (COURANT / all_max(fastest(cell_state))).reshape(1)
-    chosen = jnp.arange(slots, dtype=jnp.int32) == chosen_slot
-    after = jnp.where(chosen[:, None, None, None], incoming[None], cell_state)
+
+    peak = fastest(cell_state)
+    peak = jnp.maximum(peak, turned(peak, 1))
+    out_most, out_last, peak = lax.optimization_barrier(
+        (quarters(outgoing, 0, 1, 3), quarters(outgoing, 2), peak)
+    )
+    across = [(i, i ^ (count // 2)) for i in range(count)]
+    most = lax.ppermute(out_most, "box", across)
+    last = lax.ppermute(out_last, "box", across)
+    peak = level_max(peak)
+    near = [turned(peak, k) for k in range(2, levels // 2, 2)]
+    for value in near:
+        peak = jnp.maximum(peak, value)
+    final = turned(peak, levels // 2)
+    most, peak = lax.optimization_barrier((most, peak))
+
     own_start = lax.axis_index("box") * slots
     lower, upper = neighbours[:, 0], neighbours[:, 1]
     table = jnp.stack(
@@ -420,12 +509,20 @@
         ],
         axis=1,
     )
-    below = shifted(after[:, :, -GHOST:], 1)
-    above = shifted(after[:, :, :GHOST], -1)
-    first = line_sweep(1, table, ratio, after, below, above, plane_sweeps(after))
+    outer = jnp.where(chosen, quarters(most, 0, 2)[None], quarters(cell_state, 0, 3))
+    second = jnp.where(chosen, quarters(most, 1)[None], quarters(cell_state, 1))
+    below = shifted(outer[:, :, -GHOST:], 1)
+    above = shifted(outer[:, :, :GHOST], -1)
+    planes = [plane_sweeps(outer), plane_sweeps(second)]
+    last, *planes = lax.optimization_barrier((last, *planes))
+    third = jnp.where(chosen, last[None], quarters(cell_state, 2))
+    planes.append(plane_sweeps(third))
+    ratio = (COURANT / jnp.max(jnp.maximum(peak, final))).reshape(1)
+    after = (outer, second, third)
+    first = line_sweep(table, ratio, below, above, after, planes)
     below = shifted(first[:, :, -GHOST:], 1)
     above = shifted(first[:, :, :GHOST], -1)
-    return line_sweep(2, table, ratio, first, below, above, plane_sweeps(first), after)
+    return line_sweep(table, ratio, below, above, (first,), (plane_sweeps(first),), after)
 
 
 def solution(mesh):

time: 173 us -> 142 us (0.82)
  the two profiles are of different devices: /device:TPU:1 before, /device:TPU:191 now
where the time goes in v2:
time: 142 us; the launch traced here: 141 us
  starting transfers between devices  70.5 us (50%)
  Pallas kernels  39.1 us (28%)
  blocking collectives  24.3 us (17%)
  local copies, waits for them, and re-layouts  2.99 us (2%)
  other arithmetic  2.18 us (2%)
  between operations  1.65 us (1%)
    ppermute x5, starting transfers between devices, turned(): lax.ppermute(value, 'box', [(i, (i + levels * LEVEL) % count) for i in ra...  37.4 us
    pallas_call x4, Pallas kernels, plane_sweeps(): pl.pallas_call(functools.partial(plane_kernel, rows), out_shape=jax.Shape...  24.7 us
    all_gather x1, blocking collectives, level_max(): lax.all_gather(value, 'box', axis_index_groups=level)  24.3 us
    ppermute x4, starting transfers between devices, shifted(): lax.ppermute(value, 'box', [(s, s + steps) for s in range(first, last)])  19.6 us
    pallas_call x2, Pallas kernels, line_sweep(): pl.pallas_call(functools.partial(line_kernel, (len(state), len(plane), le...  13.7 us
    ppermute x1, starting transfers between devices, body(): most = lax.ppermute(out_most, 'box', across)  8.84 us
    ppermute x1, starting transfers between devices, body(): last = lax.ppermute(out_last, 'box', across)  4.65 us
  transfers between devices with their start and end apart: 11, of which 1 were waited for; matrix products, arithmetic and copies ran while one was open for 3% of the time, Pallas kernels for 18%

profile of v2, /device:TPU:191, one launch (start us, length us, event | category | flops | bytes accessed | tf_op | source)
XLA Modules:
  0.0 141.2 jit_solution(381993893460136854)
XLA Ops:
  0.0 0.0 copy-start
  0.0 1.3 copy-done
  1.3 0.0 copy-start.1
  1.3 0.7 fastest.1
  2.0 3.5 %collective-permute-start = (f32[8,128]{1,0:T(8,128)S(1)}, f32[8,128]{1,0:T(8,128)S(1)}, u32[]{:S(2)}, u32[]{:S(2)}) collective-permute-start(f32[8,128]{1,0:T(8,128)S(1)} %fastest.1), channel_id=1, source_target_pairs={{0,32},{1,33},{2,34},{3,35},{4,36},{5,37},{6,38},{7,39},{8,40},{9,... | collective-permute-start | bytes 12296 | tf_op jit(solution)/shard_map/ppermute | solution.py:470
  6.2 0.0 copy-done.1
  6.2 0.0 copy-start.2
  6.2 0.1 dynamic-slice_bitcast_fusion
  6.3 0.7 fusion.2
  7.0 0.0 copy-done.2
  7.0 0.1 compare_convert_fusion.1
  7.1 0.1 add_clamp_fusion.1
  7.2 0.0 collective-permute-done
  7.2 8.8 %collective-permute-start.1 = (f32[5,24,1024]{2,1,0:T(8,128)S(1)}, f32[5,24,1024]{2,1,0:T(8,128)S(1)}, u32[]{:S(2)}, u32[]{:S(2)}) collective-permute-start(f32[5,24,1024]{2,1,0:T(8,128)S(1)} %pad_maximum_fusion), channel_id=1, source_target_pairs={{0,256},{1,257},{2,258},{3,259},{4,260},{5,261},{6,262},{7,263},{8... | collective-permute-start | bytes 1474568 | tf_op jit(solution)/shard_map/ppermute | solution.py:492
  16.1 0.1 pad_add_fusion.slot_ref
  16.2 24.3 %all-gather = f32[256,128]{1,0:T(8,128)S(1)} all-gather(f32[8,128]{1,0:T(8,128)S(1)} %max.24), channel_id=2, replica_groups={{0,1,2,3,4,5,6,7,8,9,10,11,12,13,14,15,16,17,18,19,20,21,22,23,24,25,26..., dimensions={0}, use_global_device_ids=true | all-gather | bytes 135168 | tf_op jit(solution)/shard_map/all_gather | solution.py:465
  40.5 1.9 %collective-permute-start.4 = (f32[8,128]{1,0:T(8,128)S(1)}, f32[8,128]{1,0:T(8,128)S(1)}, u32[]{:S(2)}, u32[]{:S(2)}) collective-permute-start(f32[8,128]{1,0:T(8,128)S(1)} %bitcast_reduce_fusion), channel_id=1, source_target_pairs={{0,192},{1,193},{2,194},{3,195},{4,196},{5,197},{6,198},{7,199},{8... | collective-permute-start | bytes 12296 | tf_op jit(solution)/shard_map/ppermute | solution.py:470
  42.4 8.5 %collective-permute-start.3 = (f32[8,128]{1,0:T(8,128)S(1)}, f32[8,128]{1,0:T(8,128)S(1)}, u32[]{:S(2)}, u32[]{:S(2)}) collective-permute-start(f32[8,128]{1,0:T(8,128)S(1)} %bitcast_reduce_fusion), channel_id=1, source_target_pairs={{0,128},{1,129},{2,130},{3,131},{4,132},{5,133},{6,134},{7,135},{8... | collective-permute-start | bytes 12296 | tf_op jit(solution)/shard_map/ppermute | solution.py:470
  50.9 4.0 %collective-permute-start.2 = (f32[8,128]{1,0:T(8,128)S(1)}, f32[8,128]{1,0:T(8,128)S(1)}, u32[]{:S(2)}, u32[]{:S(2)}) collective-permute-start(f32[8,128]{1,0:T(8,128)S(1)} %bitcast_reduce_fusion), channel_id=1, source_target_pairs={{0,64},{1,65},{2,66},{3,67},{4,68},{5,69},{6,70},{7,71},{8,72},{9,... | collective-permute-start | bytes 12296 | tf_op jit(solution)/shard_map/ppermute | solution.py:470
  54.9 4.7 %collective-permute-start.8 = (f32[5,8,1024]{2,1,0:T(8,128)}, f32[5,8,1024]{2,1,0:T(8,128)}, u32[]{:S(2)}, u32[]{:S(2)}) collective-permute-start(f32[5,8,1024]{2,1,0:T(8,128)} %get-tuple-element.17), channel_id=1, source_target_pairs={{0,256},{1,257},{2,258},{3,259},{4,260},{5,261},{6,262},{7,263},{8... | collective-permute-start | bytes 491528 | tf_op jit(solution)/shard_map/ppermute | solution.py:493
  59.5 0.0 collective-permute-done.4
  59.5 0.0 collective-permute-done.3
  59.5 0.5 collective-permute-done.2
  60.1 19.5 %collective-permute-start.5 = (f32[8,128]{1,0:T(8,128)S(1)}, f32[8,128]{1,0:T(8,128)S(1)}, u32[]{:S(2)}, u32[]{:S(2)}) collective-permute-start(f32[8,128]{1,0:T(8,128)S(1)} %maximum_maximum_fusion), channel_id=1, source_target_pairs={{0,256},{1,257},{2,258},{3,259},{4,260},{5,261},{6,262},{7,263},{8... | collective-permute-start | bytes 12296 | tf_op jit(solution)/shard_map/ppermute | solution.py:470
  79.6 0.0 collective-permute-done.1
  79.7 0.1 slice_select_fusion.1
  79.8 0.1 maximum_select_fusion.state_ref.refs_0_.refs_2_
  79.9 0.8 fusion.1
  80.7 2.5 %collective-permute-start.7 = (f32[2,5,4,1024]{3,2,1,0:T(4,128)}, f32[2,5,4,1024]{3,2,1,0:T(4,128)S(1)}, u32[]{:S(2)}, u32[]{:S(2)}) collective-permute-start(f32[2,5,4,1024]{3,2,1,0:T(4,128)} %get-tuple-element.26), channel_id=1, source_target_pairs={{1,0},{2,1},{3,2},{4,3},{5,4},{6,5},{7,6},{8,7},{9,8},{10,9},{11,1... | collective-permute-start | bytes 491528 | tf_op jit(solution)/shard_map/ppermute | solution.py:458
  83.2 7.3 %collective-permute-start.6 = (f32[2,5,4,1024]{3,2,1,0:T(4,128)}, f32[2,5,4,1024]{3,2,1,0:T(4,128)}, u32[]{:S(2)}, u32[]{:S(2)}) collective-permute-start(f32[2,5,4,1024]{3,2,1,0:T(4,128)} %get-tuple-element.27), channel_id=1, source_target_pairs={{0,1},{1,2},{2,3},{3,4},{4,5},{5,6},{6,7},{7,8},{8,9},{9,10},{10,1... | collective-permute-start | bytes 491528 | tf_op jit(solution)/shard_map/ppermute | solution.py:458
  90.5 3.1 %plane.5.refs_4_ = f32[2,5,8,1024]{3,2,1,0:T(8,128)S(1)} custom-call(f32[2,5,8,1024]{3,2,1,0:T(8,128)S(1)} %get-tuple-element.23.state_ref.refs_1_.refs_3_), custom_call_target="tpu_custom_call" | custom-call | flops 16000000 | bytes 720000 | tf_op jit(solution)/shard_map/plane/pallas_call | solution.py:420
  93.6 6.2 %plane.4.refs_3_ = f32[2,5,16,1024]{3,2,1,0:T(8,128)S(1)} custom-call(f32[2,5,16,1024]{3,2,1,0:T(8,128)S(1)} %maximum_select_fusion.state_ref.refs_0_.refs_2_), custom_call_target="tpu_custom_call" | custom-call | flops 32000000 | bytes 1440000 | tf_op jit(solution)/shard_map/plane/pallas_call | solution.py:420
  99.9 0.0 collective-permute-done.8
  99.9 0.0 collective-permute-done.5
  99.9 0.6 maximum_reduce_fusion
  101.2 1.0 slice_select_fusion.state_ref.refs_2_.refs_4_
  102.2 3.1 %plane.6.refs_5_ = f32[2,5,8,1024]{3,2,1,0:T(8,128)S(1)} custom-call(f32[2,5,8,1024]{3,2,1,0:T(8,128)S(1)} %slice_select_fusion.state_ref.refs_2_.refs_4_), custom_call_target="tpu_custom_call" | custom-call | flops 16000000 | bytes 720000 | tf_op jit(solution)/shard_map/plane/pallas_call | solution.py:420
  105.3 0.0 collective-permute-done.7.above_ref
  105.3 0.0 collective-permute-done.6.below_ref
  105.3 6.4 %line.2.state_ref.refs_0_ = f32[2,5,32,1024]{3,2,1,0:T(8,128)S(1)} custom-call(s32[2,4]{1,0:T(2,128)S(1)} %pad_add_fusion.slot_ref, f32[1]{0:T(128)} %bitcast.3.ratio_ref, f32[2,5,4,1024]{3,2,1,0:T(4,128)} %collective-permute-done.6.below_ref, f32[2,5,4,1024]{3,2,1,0:T(4,128)S(1)} %collective-permute-done.7.above_ref, ...), custom_call_target="tpu_custom_call" | custom-call | flops 30000000 | bytes 4000000 | tf_op jit(solution)/shard_map/line/pallas_call | solution.py:441
  111.8 0.1 fusion
  111.8 1.9 %collective-permute-start.10 = (f32[2,5,4,1024]{3,2,1,0:T(4,128)S(1)}, f32[2,5,4,1024]{3,2,1,0:T(4,128)S(1)}, u32[]{:S(2)}, u32[]{:S(2)}) collective-permute-start(f32[2,5,4,1024]{3,2,1,0:T(4,128)S(1)} %get-tuple-element.21), channel_id=1, source_target_pairs={{1,0},{2,1},{3,2},{4,3},{5,4},{6,5},{7,6},{8,7},{9,8},{10,9},{11,1... | collective-permute-start | bytes 491528 | tf_op jit(solution)/shard_map/ppermute | solution.py:458
  113.8 7.9 %collective-permute-start.9 = (f32[2,5,4,1024]{3,2,1,0:T(4,128)S(1)}, f32[2,5,4,1024]{3,2,1,0:T(4,128)S(1)}, u32[]{:S(2)}, u32[]{:S(2)}) collective-permute-start(f32[2,5,4,1024]{3,2,1,0:T(4,128)S(1)} %get-tuple-element.22), channel_id=1, source_target_pairs={{0,1},{1,2},{2,3},{3,4},{4,5},{5,6},{6,7},{7,8},{8,9},{9,10},{10,1... | collective-permute-start | bytes 491528 | tf_op jit(solution)/shard_map/ppermute | solution.py:458
  121.6 12.3 %plane.7.refs_1_ = f32[2,5,32,1024]{3,2,1,0:T(8,128)S(1)} custom-call(f32[2,5,32,1024]{3,2,1,0:T(8,128)S(1)} %line.2.state_ref.refs_0_), custom_call_target="tpu_custom_call" | custom-call | flops 64000000 | bytes 2880000 | tf_op jit(solution)/shard_map/plane/pallas_call | solution.py:420
  133.9 0.0 collective-permute-done.10.above_ref
  133.9 0.0 collective-permute-done.9.below_ref
  133.9 7.3 %line.3 = f32[2,5,32,1024]{3,2,1,0:T(8,128)} custom-call(s32[2,4]{1,0:T(2,128)S(1)} %pad_add_fusion.slot_ref, f32[1]{0:T(128)} %bitcast.3.ratio_ref, f32[2,5,4,1024]{3,2,1,0:T(4,128)S(1)} %collective-permute-done.9.below_ref, f32[2,5,4,1024]{3,2,1,0:T(4,128)S(1)} %collective-permute-done.10.above_ref, f32[2,5,32,1024]{3,2,1,0:T(8,128)S(1)} %line.2.state_ref.refs_0_, ...), custom_call_target="tpu_custom_call" | custom-call | flops 30000000 | bytes 4000000 | tf_op jit(solution)/shard_map/line/pallas_call | solution.py:441
  (8 shorter events, 0.2 us)
Async XLA Ops:
  0.0 1.3 copy-start
  1.3 4.9 %copy-start.1 = (f32[2,5,32,1024]{3,2,1,0:T(8,128)S(1)}, f32[2,5,32,1024]{3,2,1,0:T(8,128)}, u32[]{:S(2)}) copy-start(f32[2,5,32,1024]{3,2,1,0:T(8,128)} %state_ref.1) | copy-start | bytes 3932164
  2.0 5.2 %collective-permute-start = (f32[8,128]{1,0:T(8,128)S(1)}, f32[8,128]{1,0:T(8,128)S(1)}, u32[]{:S(2)}, u32[]{:S(2)}) collective-permute-start(f32[8,128]{1,0:T(8,128)S(1)} %fastest.1), channel_id=1, source_target_pairs={{0,32},{1,33},{2,34},{3,35},{4,36},{5,37},{6,38},{7,39},{8,40},{9,... | collective-permute-start | bytes 12296 | tf_op jit(solution)/shard_map/ppermute | solution.py:470
  6.2 0.8 copy-start.2
  7.2 72.4 %collective-permute-start.1 = (f32[5,24,1024]{2,1,0:T(8,128)S(1)}, f32[5,24,1024]{2,1,0:T(8,128)S(1)}, u32[]{:S(2)}, u32[]{:S(2)}) collective-permute-start(f32[5,24,1024]{2,1,0:T(8,128)S(1)} %pad_maximum_fusion), channel_id=1, source_target_pairs={{0,256},{1,257},{2,258},{3,259},{4,260},{5,261},{6,262},{7,263},{8... | collective-permute-start | bytes 1474568 | tf_op jit(solution)/shard_map/ppermute | solution.py:492
  40.5 19.1 %collective-permute-start.4 = (f32[8,128]{1,0:T(8,128)S(1)}, f32[8,128]{1,0:T(8,128)S(1)}, u32[]{:S(2)}, u32[]{:S(2)}) collective-permute-start(f32[8,128]{1,0:T(8,128)S(1)} %bitcast_reduce_fusion), channel_id=1, source_target_pairs={{0,192},{1,193},{2,194},{3,195},{4,196},{5,197},{6,198},{7,199},{8... | collective-permute-start | bytes 12296 | tf_op jit(solution)/shard_map/ppermute | solution.py:470
  42.4 17.1 %collective-permute-start.3 = (f32[8,128]{1,0:T(8,128)S(1)}, f32[8,128]{1,0:T(8,128)S(1)}, u32[]{:S(2)}, u32[]{:S(2)}) collective-permute-start(f32[8,128]{1,0:T(8,128)S(1)} %bitcast_reduce_fusion), channel_id=1, source_target_pairs={{0,128},{1,129},{2,130},{3,131},{4,132},{5,133},{6,134},{7,135},{8... | collective-permute-start | bytes 12296 | tf_op jit(solution)/shard_map/ppermute | solution.py:470
  50.9 9.2 %collective-permute-start.2 = (f32[8,128]{1,0:T(8,128)S(1)}, f32[8,128]{1,0:T(8,128)S(1)}, u32[]{:S(2)}, u32[]{:S(2)}) collective-permute-start(f32[8,128]{1,0:T(8,128)S(1)} %bitcast_reduce_fusion), channel_id=1, source_target_pairs={{0,64},{1,65},{2,66},{3,67},{4,68},{5,69},{6,70},{7,71},{8,72},{9,... | collective-permute-start | bytes 12296 | tf_op jit(solution)/shard_map/ppermute | solution.py:470
  54.9 45.0 %collective-permute-start.8 = (f32[5,8,1024]{2,1,0:T(8,128)}, f32[5,8,1024]{2,1,0:T(8,128)}, u32[]{:S(2)}, u32[]{:S(2)}) collective-permute-start(f32[5,8,1024]{2,1,0:T(8,128)} %get-tuple-element.17), channel_id=1, source_target_pairs={{0,256},{1,257},{2,258},{3,259},{4,260},{5,261},{6,262},{7,263},{8... | collective-permute-start | bytes 491528 | tf_op jit(solution)/shard_map/ppermute | solution.py:493
  60.1 39.8 %collective-permute-start.5 = (f32[8,128]{1,0:T(8,128)S(1)}, f32[8,128]{1,0:T(8,128)S(1)}, u32[]{:S(2)}, u32[]{:S(2)}) collective-permute-start(f32[8,128]{1,0:T(8,128)S(1)} %maximum_maximum_fusion), channel_id=1, source_target_pairs={{0,256},{1,257},{2,258},{3,259},{4,260},{5,261},{6,262},{7,263},{8... | collective-permute-start | bytes 12296 | tf_op jit(solution)/shard_map/ppermute | solution.py:470
  80.7 24.6 %collective-permute-start.7 = (f32[2,5,4,1024]{3,2,1,0:T(4,128)}, f32[2,5,4,1024]{3,2,1,0:T(4,128)S(1)}, u32[]{:S(2)}, u32[]{:S(2)}) collective-permute-start(f32[2,5,4,1024]{3,2,1,0:T(4,128)} %get-tuple-element.26), channel_id=1, source_target_pairs={{1,0},{2,1},{3,2},{4,3},{5,4},{6,5},{7,6},{8,7},{9,8},{10,9},{11,1... | collective-permute-start | bytes 491528 | tf_op jit(solution)/shard_map/ppermute | solution.py:458
  83.2 22.1 %collective-permute-start.6 = (f32[2,5,4,1024]{3,2,1,0:T(4,128)}, f32[2,5,4,1024]{3,2,1,0:T(4,128)}, u32[]{:S(2)}, u32[]{:S(2)}) collective-permute-start(f32[2,5,4,1024]{3,2,1,0:T(4,128)} %get-tuple-element.27), channel_id=1, source_target_pairs={{0,1},{1,2},{2,3},{3,4},{4,5},{5,6},{6,7},{7,8},{8,9},{9,10},{10,1... | collective-permute-start | bytes 491528 | tf_op jit(solution)/shard_map/ppermute | solution.py:458
  111.8 22.1 %collective-permute-start.10 = (f32[2,5,4,1024]{3,2,1,0:T(4,128)S(1)}, f32[2,5,4,1024]{3,2,1,0:T(4,128)S(1)}, u32[]{:S(2)}, u32[]{:S(2)}) collective-permute-start(f32[2,5,4,1024]{3,2,1,0:T(4,128)S(1)} %get-tuple-element.21), channel_id=1, source_target_pairs={{1,0},{2,1},{3,2},{4,3},{5,4},{6,5},{7,6},{8,7},{9,8},{10,9},{11,1... | collective-permute-start | bytes 491528 | tf_op jit(solution)/shard_map/ppermute | solution.py:458
  113.8 20.1 %collective-permute-start.9 = (f32[2,5,4,1024]{3,2,1,0:T(4,128)S(1)}, f32[2,5,4,1024]{3,2,1,0:T(4,128)S(1)}, u32[]{:S(2)}, u32[]{:S(2)}) collective-permute-start(f32[2,5,4,1024]{3,2,1,0:T(4,128)S(1)} %get-tuple-element.22), channel_id=1, source_target_pairs={{0,1},{1,2},{2,3},{3,4},{4,5},{5,6},{6,7},{7,8},{8,9},{9,10},{10,1... | collective-permute-start | bytes 491528 | tf_op jit(solution)/shard_map/ppermute | solution.py:458

commit v3 on v2

--- a/solution.py
+++ b/solution.py
@@ -22,8 +22,7 @@
 
 
 def rcp(value):
-    guess = pl.reciprocal(value, approx=True)
-    return guess * (2.0 - value * guess)
+    return 1.0 / value
 
 
 def prims_of(cons):
@@ -165,7 +164,7 @@
 
     columns(fill, ratio)
 
-    def turn_in(quad, _):
+    def turn_in(quad):
         for f in range(5):
             turned = prim[f, pl.ds(quad * joined, joined)].reshape(128, 128).T
             for k in range(4):
@@ -173,9 +172,6 @@
                 zprim[f, pl.ds(start + 8, BZC)] = turned[BZC * k : BZC * (k + 1)]
                 zprim[f, pl.ds(start + 6, 2)] = zprim[f, pl.ds(start + 38, 2)]
                 zprim[f, pl.ds(start + 40, 2)] = zprim[f, pl.ds(start + 8, 2)]
-        return 0
-
-    lax.fori_loop(0, COLS // joined, turn_in, 0)
 
     def y_faces(tile):
         for f in range(5):
@@ -222,7 +218,15 @@
 
         lax.fori_loop(0, COLS // ratio, turn, 0)
 
-    both(y_faces, z_faces)
+    quads = COLS // joined
+
+    def turn_and_y_faces(quad, _):
+        turn_in(quad)
+        for k in range(joined):
+            y_faces(quad * joined + k)
+        return 0
+
+    lax.fori_loop(0, quads, turn_and_y_faces, 0)
 
     def y_states(tile):
         get = lambda t: shock[t]
@@ -250,7 +254,7 @@
             zlow[f, pl.ds(start + 40, 1)] = lower[:1]
             zhigh[f, pl.ds(start + 8, BZC)] = upper
 
-    both(y_states, z_states)
+    both(y_states, z_faces)
 
     def y_flux(tile):
         left = [high[f, tile] for f in range(5)]
@@ -268,9 +272,13 @@
             zflux[f, pl.ds(start + 8, BZC)] = values[f]
             zflux[f, pl.ds(start + 7, 1)] = values[f][BZC - 1 :]
 
-    both(y_flux, z_flux)
-
-    def turn_out(quad, _):
+    both(y_flux, z_states)
+
+    def z_fluxes(quad):
+        for k in range(4):
+            z_flux(quad * 4 + k)
+
+    def turn_out(quad):
         for f in range(5):
             across = []
             for k in range(4):
@@ -283,9 +291,15 @@
                 lanes = pl.ds(pl.multiple_of(part * 128, 128), 128)
                 along = flux[f, tile] - y_back(lambda t, f=f: flux[f, t], tile, 1)
                 out_ref[box, f, :, lanes] = along + turned[rows * k : rows * (k + 1)]
+
+    def solve_and_turn(quad, _):
+        turn_out(quad - 1)
+        z_fluxes(quad)
         return 0
 
-    lax.fori_loop(0, COLS // joined, turn_out, 0)
+    z_fluxes(0)
+    lax.fori_loop(1, quads, solve_and_turn, 0)
+    turn_out(quads - 1)
 
 
 def whole(refs, box, field, lanes):

time: 142 us -> 138 us (0.972)
  Pallas kernels: 39.1 us -> 35.7 us
    pallas_call x4, Pallas kernels: 24.7 us -> 22.2 us  [plane_sweeps(): pl.pallas_call(functools.partial(plane_kernel, rows), out_shape=jax.Shape...]
  transfers between devices with their start and end apart: 11 -> 11, of which waited for: 1 -> 1; matrix products, arithmetic and copies ran while one was open for 3% -> 3% of each run, Pallas kernels for 18% -> 16%
where the time goes in v3:
time: 138 us
  starting transfers between devices  70.5 us (51%)
  Pallas kernels  35.7 us (26%)
  blocking collectives  24.3 us (18%)
  local copies, waits for them, and re-layouts  2.99 us (2%)
  other arithmetic  2.18 us (2%)
  between operations  1.65 us (1%)
    ppermute x5, starting transfers between devices, turned(): lax.ppermute(value, 'box', [(i, (i + levels * LEVEL) % count) for i in ra...  37.4 us
    all_gather x1, blocking collectives, level_max(): lax.all_gather(value, 'box', axis_index_groups=level)  24.3 us
    pallas_call x4, Pallas kernels, plane_sweeps(): pl.pallas_call(functools.partial(plane_kernel, rows), out_shape=jax.Shape...  22.2 us
    ppermute x4, starting transfers between devices, shifted(): lax.ppermute(value, 'box', [(s, s + steps) for s in range(first, last)])  19.6 us
    pallas_call x2, Pallas kernels, line_sweep(): pl.pallas_call(functools.partial(line_kernel, (len(state), len(plane), le...  12.9 us
    ppermute x1, starting transfers between devices, body(): most = lax.ppermute(out_most, 'box', across)  8.84 us
    ppermute x1, starting transfers between devices, body(): last = lax.ppermute(out_last, 'box', across)  4.65 us
  transfers between devices with their start and end apart: 11, of which 1 were waited for; matrix products, arithmetic and copies ran while one was open for 3% of the time, Pallas kernels for 16%

profile of v3, /device:TPU:191, one launch (start us, length us, event | category | flops | bytes accessed | tf_op | source)
XLA Modules:
  0.0 137.8 jit_solution(6806612309839411339)
XLA Ops:
  0.0 0.0 copy-start
  0.0 1.3 copy-done
  1.3 0.0 copy-start.1
  1.3 0.6 fastest.1
  2.0 3.5 %collective-permute-start = (f32[8,128]{1,0:T(8,128)S(1)}, f32[8,128]{1,0:T(8,128)S(1)}, u32[]{:S(2)}, u32[]{:S(2)}) collective-permute-start(f32[8,128]{1,0:T(8,128)S(1)} %fastest.1), channel_id=1, source_target_pairs={{0,32},{1,33},{2,34},{3,35},{4,36},{5,37},{6,38},{7,39},{8,40},{9,... | collective-permute-start | bytes 12296 | tf_op jit(solution)/shard_map/ppermute | solution.py:484
  6.2 0.0 copy-done.1
  6.2 0.0 copy-start.2
  6.2 0.1 dynamic-slice_bitcast_fusion
  6.3 0.7 fusion.2
  7.0 0.0 copy-done.2
  7.0 0.1 compare_convert_fusion.1
  7.1 0.1 add_clamp_fusion.1
  7.2 0.0 collective-permute-done
  7.2 8.8 %collective-permute-start.1 = (f32[5,24,1024]{2,1,0:T(8,128)S(1)}, f32[5,24,1024]{2,1,0:T(8,128)S(1)}, u32[]{:S(2)}, u32[]{:S(2)}) collective-permute-start(f32[5,24,1024]{2,1,0:T(8,128)S(1)} %pad_maximum_fusion), channel_id=1, source_target_pairs={{0,256},{1,257},{2,258},{3,259},{4,260},{5,261},{6,262},{7,263},{8... | collective-permute-start | bytes 1474568 | tf_op jit(solution)/shard_map/ppermute | solution.py:506
  16.0 0.1 pad_add_fusion.slot_ref
  16.1 24.3 %all-gather = f32[256,128]{1,0:T(8,128)S(1)} all-gather(f32[8,128]{1,0:T(8,128)S(1)} %max.24), channel_id=2, replica_groups={{0,1,2,3,4,5,6,7,8,9,10,11,12,13,14,15,16,17,18,19,20,21,22,23,24,25,26..., dimensions={0}, use_global_device_ids=true | all-gather | bytes 135168 | tf_op jit(solution)/shard_map/all_gather | solution.py:479
  40.4 1.9 %collective-permute-start.4 = (f32[8,128]{1,0:T(8,128)S(1)}, f32[8,128]{1,0:T(8,128)S(1)}, u32[]{:S(2)}, u32[]{:S(2)}) collective-permute-start(f32[8,128]{1,0:T(8,128)S(1)} %bitcast_reduce_fusion), channel_id=1, source_target_pairs={{0,192},{1,193},{2,194},{3,195},{4,196},{5,197},{6,198},{7,199},{8... | collective-permute-start | bytes 12296 | tf_op jit(solution)/shard_map/ppermute | solution.py:484
  42.3 8.5 %collective-permute-start.3 = (f32[8,128]{1,0:T(8,128)S(1)}, f32[8,128]{1,0:T(8,128)S(1)}, u32[]{:S(2)}, u32[]{:S(2)}) collective-permute-start(f32[8,128]{1,0:T(8,128)S(1)} %bitcast_reduce_fusion), channel_id=1, source_target_pairs={{0,128},{1,129},{2,130},{3,131},{4,132},{5,133},{6,134},{7,135},{8... | collective-permute-start | bytes 12296 | tf_op jit(solution)/shard_map/ppermute | solution.py:484
  50.8 4.0 %collective-permute-start.2 = (f32[8,128]{1,0:T(8,128)S(1)}, f32[8,128]{1,0:T(8,128)S(1)}, u32[]{:S(2)}, u32[]{:S(2)}) collective-permute-start(f32[8,128]{1,0:T(8,128)S(1)} %bitcast_reduce_fusion), channel_id=1, source_target_pairs={{0,64},{1,65},{2,66},{3,67},{4,68},{5,69},{6,70},{7,71},{8,72},{9,... | collective-permute-start | bytes 12296 | tf_op jit(solution)/shard_map/ppermute | solution.py:484
  54.8 4.7 %collective-permute-start.8 = (f32[5,8,1024]{2,1,0:T(8,128)}, f32[5,8,1024]{2,1,0:T(8,128)}, u32[]{:S(2)}, u32[]{:S(2)}) collective-permute-start(f32[5,8,1024]{2,1,0:T(8,128)} %get-tuple-element.17), channel_id=1, source_target_pairs={{0,256},{1,257},{2,258},{3,259},{4,260},{5,261},{6,262},{7,263},{8... | collective-permute-start | bytes 491528 | tf_op jit(solution)/shard_map/ppermute | solution.py:507
  59.5 0.0 collective-permute-done.4
  59.5 0.0 collective-permute-done.3
  59.5 0.5 collective-permute-done.2
  60.0 19.5 %collective-permute-start.5 = (f32[8,128]{1,0:T(8,128)S(1)}, f32[8,128]{1,0:T(8,128)S(1)}, u32[]{:S(2)}, u32[]{:S(2)}) collective-permute-start(f32[8,128]{1,0:T(8,128)S(1)} %maximum_maximum_fusion), channel_id=1, source_target_pairs={{0,256},{1,257},{2,258},{3,259},{4,260},{5,261},{6,262},{7,263},{8... | collective-permute-start | bytes 12296 | tf_op jit(solution)/shard_map/ppermute | solution.py:484
  79.6 0.0 collective-permute-done.1
  79.6 0.1 slice_select_fusion.1
  79.7 0.1 maximum_select_fusion.state_ref.refs_0_.refs_2_
  79.9 0.8 fusion.1
  80.7 2.5 %collective-permute-start.7 = (f32[2,5,4,1024]{3,2,1,0:T(4,128)}, f32[2,5,4,1024]{3,2,1,0:T(4,128)S(1)}, u32[]{:S(2)}, u32[]{:S(2)}) collective-permute-start(f32[2,5,4,1024]{3,2,1,0:T(4,128)} %get-tuple-element.26), channel_id=1, source_target_pairs={{1,0},{2,1},{3,2},{4,3},{5,4},{6,5},{7,6},{8,7},{9,8},{10,9},{11,1... | collective-permute-start | bytes 491528 | tf_op jit(solution)/shard_map/ppermute | solution.py:472
  83.2 7.3 %collective-permute-start.6 = (f32[2,5,4,1024]{3,2,1,0:T(4,128)}, f32[2,5,4,1024]{3,2,1,0:T(4,128)}, u32[]{:S(2)}, u32[]{:S(2)}) collective-permute-start(f32[2,5,4,1024]{3,2,1,0:T(4,128)} %get-tuple-element.27), channel_id=1, source_target_pairs={{0,1},{1,2},{2,3},{3,4},{4,5},{5,6},{6,7},{7,8},{8,9},{9,10},{10,1... | collective-permute-start | bytes 491528 | tf_op jit(solution)/shard_map/ppermute | solution.py:472
  90.5 2.9 %plane.5.refs_4_ = f32[2,5,8,1024]{3,2,1,0:T(8,128)S(1)} custom-call(f32[2,5,8,1024]{3,2,1,0:T(8,128)S(1)} %get-tuple-element.23.state_ref.refs_1_.refs_3_), custom_call_target="tpu_custom_call" | custom-call | flops 16000000 | bytes 720000 | tf_op jit(solution)/shard_map/plane/pallas_call | solution.py:434
  93.3 5.5 %plane.4.refs_3_ = f32[2,5,16,1024]{3,2,1,0:T(8,128)S(1)} custom-call(f32[2,5,16,1024]{3,2,1,0:T(8,128)S(1)} %maximum_select_fusion.state_ref.refs_0_.refs_2_), custom_call_target="tpu_custom_call" | custom-call | flops 32000000 | bytes 1440000 | tf_op jit(solution)/shard_map/plane/pallas_call | solution.py:434
  98.8 0.0 collective-permute-done.8
  98.8 0.0 collective-permute-done.5
  98.9 0.6 maximum_reduce_fusion
  100.2 1.0 slice_select_fusion.state_ref.refs_2_.refs_4_
  101.2 2.9 %plane.6.refs_5_ = f32[2,5,8,1024]{3,2,1,0:T(8,128)S(1)} custom-call(f32[2,5,8,1024]{3,2,1,0:T(8,128)S(1)} %slice_select_fusion.state_ref.refs_2_.refs_4_), custom_call_target="tpu_custom_call" | custom-call | flops 16000000 | bytes 720000 | tf_op jit(solution)/shard_map/plane/pallas_call | solution.py:434
  104.0 0.0 collective-permute-done.7.above_ref
  104.0 0.0 collective-permute-done.6.below_ref
  104.1 6.0 %line.2.state_ref.refs_0_ = f32[2,5,32,1024]{3,2,1,0:T(8,128)S(1)} custom-call(s32[2,4]{1,0:T(2,128)S(1)} %pad_add_fusion.slot_ref, f32[1]{0:T(128)} %bitcast.3.ratio_ref, f32[2,5,4,1024]{3,2,1,0:T(4,128)} %collective-permute-done.6.below_ref, f32[2,5,4,1024]{3,2,1,0:T(4,128)S(1)} %collective-permute-done.7.above_ref, ...), custom_call_target="tpu_custom_call" | custom-call | flops 30000000 | bytes 4000000 | tf_op jit(solution)/shard_map/line/pallas_call | solution.py:455
  110.0 0.1 fusion
  110.1 1.9 %collective-permute-start.10 = (f32[2,5,4,1024]{3,2,1,0:T(4,128)S(1)}, f32[2,5,4,1024]{3,2,1,0:T(4,128)S(1)}, u32[]{:S(2)}, u32[]{:S(2)}) collective-permute-start(f32[2,5,4,1024]{3,2,1,0:T(4,128)S(1)} %get-tuple-element.21), channel_id=1, source_target_pairs={{1,0},{2,1},{3,2},{4,3},{5,4},{6,5},{7,6},{8,7},{9,8},{10,9},{11,1... | collective-permute-start | bytes 491528 | tf_op jit(solution)/shard_map/ppermute | solution.py:472
  112.0 7.9 %collective-permute-start.9 = (f32[2,5,4,1024]{3,2,1,0:T(4,128)S(1)}, f32[2,5,4,1024]{3,2,1,0:T(4,128)S(1)}, u32[]{:S(2)}, u32[]{:S(2)}) collective-permute-start(f32[2,5,4,1024]{3,2,1,0:T(4,128)S(1)} %get-tuple-element.22), channel_id=1, source_target_pairs={{0,1},{1,2},{2,3},{3,4},{4,5},{5,6},{6,7},{7,8},{8,9},{9,10},{10,1... | collective-permute-start | bytes 491528 | tf_op jit(solution)/shard_map/ppermute | solution.py:472
  119.9 10.9 %plane.7.refs_1_ = f32[2,5,32,1024]{3,2,1,0:T(8,128)S(1)} custom-call(f32[2,5,32,1024]{3,2,1,0:T(8,128)S(1)} %line.2.state_ref.refs_0_), custom_call_target="tpu_custom_call" | custom-call | flops 64000000 | bytes 2880000 | tf_op jit(solution)/shard_map/plane/pallas_call | solution.py:434
  130.9 0.0 collective-permute-done.10.above_ref
  130.9 0.0 collective-permute-done.9.below_ref
  130.9 6.9 %line.3 = f32[2,5,32,1024]{3,2,1,0:T(8,128)} custom-call(s32[2,4]{1,0:T(2,128)S(1)} %pad_add_fusion.slot_ref, f32[1]{0:T(128)} %bitcast.3.ratio_ref, f32[2,5,4,1024]{3,2,1,0:T(4,128)S(1)} %collective-permute-done.9.below_ref, f32[2,5,4,1024]{3,2,1,0:T(4,128)S(1)} %collective-permute-done.10.above_ref, f32[2,5,32,1024]{3,2,1,0:T(8,128)S(1)} %line.2.state_ref.refs_0_, ...), custom_call_target="tpu_custom_call" | custom-call | flops 30000000 | bytes 4000000 | tf_op jit(solution)/shard_map/line/pallas_call | solution.py:455
  (8 shorter events, 0.2 us)
Async XLA Ops:
  0.0 1.3 copy-start
  1.3 4.9 %copy-start.1 = (f32[2,5,32,1024]{3,2,1,0:T(8,128)S(1)}, f32[2,5,32,1024]{3,2,1,0:T(8,128)}, u32[]{:S(2)}) copy-start(f32[2,5,32,1024]{3,2,1,0:T(8,128)} %state_ref.1) | copy-start | bytes 3932164
  2.0 5.2 %collective-permute-start = (f32[8,128]{1,0:T(8,128)S(1)}, f32[8,128]{1,0:T(8,128)S(1)}, u32[]{:S(2)}, u32[]{:S(2)}) collective-permute-start(f32[8,128]{1,0:T(8,128)S(1)} %fastest.1), channel_id=1, source_target_pairs={{0,32},{1,33},{2,34},{3,35},{4,36},{5,37},{6,38},{7,39},{8,40},{9,... | collective-permute-start | bytes 12296 | tf_op jit(solution)/shard_map/ppermute | solution.py:484
  6.2 0.8 copy-start.2
  7.2 72.4 %collective-permute-start.1 = (f32[5,24,1024]{2,1,0:T(8,128)S(1)}, f32[5,24,1024]{2,1,0:T(8,128)S(1)}, u32[]{:S(2)}, u32[]{:S(2)}) collective-permute-start(f32[5,24,1024]{2,1,0:T(8,128)S(1)} %pad_maximum_fusion), channel_id=1, source_target_pairs={{0,256},{1,257},{2,258},{3,259},{4,260},{5,261},{6,262},{7,263},{8... | collective-permute-start | bytes 1474568 | tf_op jit(solution)/shard_map/ppermute | solution.py:506
  40.4 19.1 %collective-permute-start.4 = (f32[8,128]{1,0:T(8,128)S(1)}, f32[8,128]{1,0:T(8,128)S(1)}, u32[]{:S(2)}, u32[]{:S(2)}) collective-permute-start(f32[8,128]{1,0:T(8,128)S(1)} %bitcast_reduce_fusion), channel_id=1, source_target_pairs={{0,192},{1,193},{2,194},{3,195},{4,196},{5,197},{6,198},{7,199},{8... | collective-permute-start | bytes 12296 | tf_op jit(solution)/shard_map/ppermute | solution.py:484
  42.3 17.1 %collective-permute-start.3 = (f32[8,128]{1,0:T(8,128)S(1)}, f32[8,128]{1,0:T(8,128)S(1)}, u32[]{:S(2)}, u32[]{:S(2)}) collective-permute-start(f32[8,128]{1,0:T(8,128)S(1)} %bitcast_reduce_fusion), channel_id=1, source_target_pairs={{0,128},{1,129},{2,130},{3,131},{4,132},{5,133},{6,134},{7,135},{8... | collective-permute-start | bytes 12296 | tf_op jit(solution)/shard_map/ppermute | solution.py:484
  50.8 9.2 %collective-permute-start.2 = (f32[8,128]{1,0:T(8,128)S(1)}, f32[8,128]{1,0:T(8,128)S(1)}, u32[]{:S(2)}, u32[]{:S(2)}) collective-permute-start(f32[8,128]{1,0:T(8,128)S(1)} %bitcast_reduce_fusion), channel_id=1, source_target_pairs={{0,64},{1,65},{2,66},{3,67},{4,68},{5,69},{6,70},{7,71},{8,72},{9,... | collective-permute-start | bytes 12296 | tf_op jit(solution)/shard_map/ppermute | solution.py:484
  54.8 44.0 %collective-permute-start.8 = (f32[5,8,1024]{2,1,0:T(8,128)}, f32[5,8,1024]{2,1,0:T(8,128)}, u32[]{:S(2)}, u32[]{:S(2)}) collective-permute-start(f32[5,8,1024]{2,1,0:T(8,128)} %get-tuple-element.17), channel_id=1, source_target_pairs={{0,256},{1,257},{2,258},{3,259},{4,260},{5,261},{6,262},{7,263},{8... | collective-permute-start | bytes 491528 | tf_op jit(solution)/shard_map/ppermute | solution.py:507
  60.0 38.8 %collective-permute-start.5 = (f32[8,128]{1,0:T(8,128)S(1)}, f32[8,128]{1,0:T(8,128)S(1)}, u32[]{:S(2)}, u32[]{:S(2)}) collective-permute-start(f32[8,128]{1,0:T(8,128)S(1)} %maximum_maximum_fusion), channel_id=1, source_target_pairs={{0,256},{1,257},{2,258},{3,259},{4,260},{5,261},{6,262},{7,263},{8... | collective-permute-start | bytes 12296 | tf_op jit(solution)/shard_map/ppermute | solution.py:484
  80.7 23.3 %collective-permute-start.7 = (f32[2,5,4,1024]{3,2,1,0:T(4,128)}, f32[2,5,4,1024]{3,2,1,0:T(4,128)S(1)}, u32[]{:S(2)}, u32[]{:S(2)}) collective-permute-start(f32[2,5,4,1024]{3,2,1,0:T(4,128)} %get-tuple-element.26), channel_id=1, source_target_pairs={{1,0},{2,1},{3,2},{4,3},{5,4},{6,5},{7,6},{8,7},{9,8},{10,9},{11,1... | collective-permute-start | bytes 491528 | tf_op jit(solution)/shard_map/ppermute | solution.py:472
  83.2 20.9 %collective-permute-start.6 = (f32[2,5,4,1024]{3,2,1,0:T(4,128)}, f32[2,5,4,1024]{3,2,1,0:T(4,128)}, u32[]{:S(2)}, u32[]{:S(2)}) collective-permute-start(f32[2,5,4,1024]{3,2,1,0:T(4,128)} %get-tuple-element.27), channel_id=1, source_target_pairs={{0,1},{1,2},{2,3},{3,4},{4,5},{5,6},{6,7},{7,8},{8,9},{9,10},{10,1... | collective-permute-start | bytes 491528 | tf_op jit(solution)/shard_map/ppermute | solution.py:472
  110.1 20.8 %collective-permute-start.10 = (f32[2,5,4,1024]{3,2,1,0:T(4,128)S(1)}, f32[2,5,4,1024]{3,2,1,0:T(4,128)S(1)}, u32[]{:S(2)}, u32[]{:S(2)}) collective-permute-start(f32[2,5,4,1024]{3,2,1,0:T(4,128)S(1)} %get-tuple-element.21), channel_id=1, source_target_pairs={{1,0},{2,1},{3,2},{4,3},{5,4},{6,5},{7,6},{8,7},{9,8},{10,9},{11,1... | collective-permute-start | bytes 491528 | tf_op jit(solution)/shard_map/ppermute | solution.py:472
  112.0 18.8 %collective-permute-start.9 = (f32[2,5,4,1024]{3,2,1,0:T(4,128)S(1)}, f32[2,5,4,1024]{3,2,1,0:T(4,128)S(1)}, u32[]{:S(2)}, u32[]{:S(2)}) collective-permute-start(f32[2,5,4,1024]{3,2,1,0:T(4,128)S(1)} %get-tuple-element.22), channel_id=1, source_target_pairs={{0,1},{1,2},{2,3},{3,4},{4,5},{5,6},{6,7},{7,8},{8,9},{9,10},{10,1... | collective-permute-start | bytes 491528 | tf_op jit(solution)/shard_map/ppermute | solution.py:472

commit v4 on v2

--- a/solution.py
+++ b/solution.py
@@ -16,14 +16,14 @@
 TILES = 8
 COLS = 16
 QUARTER = XC // 4
+SET_ROWS = 128 // COLS
 LEVEL = 32
 PAD = 48
 F32 = jnp.float32
 
 
 def rcp(value):
-    guess = pl.reciprocal(value, approx=True)
-    return guess * (2.0 - value * guess)
+    return 1.0 / value
 
 
 def prims_of(cons):
@@ -139,153 +139,178 @@
 
 
 def plane_kernel(
-    rows, state_ref, out_ref, prim, near, far, shock, low, high, flux,
-    zprim, znear, zfar, zshock, zlow, zhigh, zflux,
+    rows, state_ref, out_ref, prim, ynear, yfar, yshock, ylow, yhigh, yflux,
+    znear, zfar, zshock, zlow, zhigh, zflux,
 ):
-    lane = lax.broadcasted_iota(jnp.int32, (rows, 128), 1)
-    joined = 128 // rows
-    ratio = XC // rows
-
-    def y_ahead(get, tile, steps):
-        nxt = lax.rem(tile + 1, COLS)
-        return pltpu.roll(
-            jnp.where(lane < 32 * steps, get(nxt), get(tile)), 128 - 32 * steps, 1
-        )
-
-    def y_back(get, tile, steps):
-        prv = lax.rem(tile + COLS - 1, COLS)
-        return pltpu.roll(jnp.where(lane >= 128 - 32 * steps, get(prv), get(tile)), 32 * steps, 1)
-
-    def fill(tile):
-        box, part = tile // TILES, tile % TILES
-        lanes = pl.ds(pl.multiple_of(part * 128, 128), 128)
-        values = prims_of([state_ref[box, f, :, lanes] for f in range(5)])
-        for f in range(5):
-            prim[f, tile] = values[f]
-
-    columns(fill, ratio)
-
-    def turn_in(quad, _):
-        for f in range(5):
-            turned = prim[f, pl.ds(quad * joined, joined)].reshape(128, 128).T
+    lane_rows = SET_ROWS
+    inside = pl.ds(8, BZC)
+
+    def follow(value):
+        return pltpu.roll(value, 128 - lane_rows, 1)
+
+    def precede(value):
+        return pltpu.roll(value, lane_rows, 1)
+
+    def strip(index):
+        steps(pl.ds(pl.multiple_of(index * lane_rows, lane_rows), lane_rows))
+
+    def tile_of(index):
+        box, part = divmod(index, TILES)
+        return box, pl.ds(part * 128, 128)
+
+    def turn_in(chosen):
+        values = []
+        for k in range(COLS):
+            box, lanes = tile_of(k)
+            values.append(prims_of([state_ref[box, f, chosen, lanes] for f in range(5)]))
+        for f in range(5):
+            swapped = jnp.concatenate([v[f] for v in values], axis=0).T
             for k in range(4):
-                start = (quad * 4 + k) * PAD
-                zprim[f, pl.ds(start + 8, BZC)] = turned[BZC * k : BZC * (k + 1)]
-                zprim[f, pl.ds(start + 6, 2)] = zprim[f, pl.ds(start + 38, 2)]
-                zprim[f, pl.ds(start + 40, 2)] = zprim[f, pl.ds(start + 8, 2)]
+                here = 2 + k
+                prim[f, here, pl.ds(8, BZC)] = swapped[BZC * k : BZC * (k + 1)]
+                prim[f, here, pl.ds(6, 2)] = swapped[BZC * (k + 1) - 2 : BZC * (k + 1)]
+                prim[f, here, pl.ds(40, 2)] = swapped[BZC * k : BZC * k + 2]
+
+    def z_faces():
+        for k in range(4):
+            here, start = 2 + k, k * PAD
+            column = prim.at[:, here]
+            for f in range(5):
+                behind, centre = column[f, pl.ds(7, BZC)], column[f, inside]
+                ahead, second = column[f, pl.ds(9, BZC)], column[f, pl.ds(10, BZC)]
+                rise, rest = face_parts(behind, centre, ahead, second)
+                znear[f, pl.ds(start + 8, BZC)] = rise
+                zfar[f, pl.ds(start + 8, BZC)] = rest
+                zfar[f, pl.ds(start + 7, 1)] = rest[BZC - 1 :]
+                if f == 3:
+                    vel_m, vel_p = behind, ahead
+                if f == 4:
+                    level = shock_of(
+                        column[f, pl.ds(6, BZC)], behind, ahead, second, vel_m, vel_p
+                    )
+                    zshock[pl.ds(start + 8, BZC)] = level
+                    zshock[pl.ds(start + 7, 1)] = level[BZC - 1 :]
+                    zshock[pl.ds(start + 40, 1)] = level[:1]
+
+    def z_states():
+        for k in range(4):
+            here, start = 2 + k, k * PAD
+            flatten = 1.0 - jnp.maximum(
+                jnp.maximum(zshock[pl.ds(start + 7, BZC)], zshock[pl.ds(start + 8, BZC)]),
+                zshock[pl.ds(start + 9, BZC)],
+            )
+            for f in range(5):
+                lower, upper = edge_states(
+                    prim[f, here, inside],
+                    zfar[f, pl.ds(start + 7, BZC)],
+                    znear[f, pl.ds(start + 8, BZC)],
+                    flatten,
+                )
+                zlow[f, pl.ds(start + 8, BZC)] = lower
+                zlow[f, pl.ds(start + 40, 1)] = lower[:1]
+                zhigh[f, pl.ds(start + 8, BZC)] = upper
+
+    def z_solves():
+        for k in range(4):
+            start = k * PAD
+            left = [zhigh[f, pl.ds(start + 8, BZC)] for f in range(5)]
+            right = [zlow[f, pl.ds(start + 9, BZC)] for f in range(5)]
+            values = riemann(left, right, 3)
+            for f in range(5):
+                zflux[f, pl.ds(start + 8, BZC)] = values[f]
+                zflux[f, pl.ds(start + 7, 1)] = values[f][BZC - 1 :]
+
+    def prim_ends():
+        for f in range(5):
+            for k in range(2):
+                prim[f, k, inside] = precede(prim[f, 4 + k, inside])
+                prim[f, 6 + k, inside] = follow(prim[f, 2 + k, inside])
+
+    def y_faces():
+        for k in range(4):
+            here = 2 + k
+            for f in range(5):
+                behind, centre = prim[f, here - 1, inside], prim[f, here, inside]
+                ahead, second = prim[f, here + 1, inside], prim[f, here + 2, inside]
+                rise, rest = face_parts(behind, centre, ahead, second)
+                ynear[f, k] = rise
+                yfar[f, 1 + k] = rest
+                if f == 2:
+                    vel_m, vel_p = behind, ahead
+                if f == 4:
+                    yshock[1 + k] = shock_of(
+                        prim[f, here - 2, inside], behind, ahead, second, vel_m, vel_p
+                    )
+
+    def face_ends():
+        for f in range(5):
+            yfar[f, 0] = precede(yfar[f, 4])
+        yshock[0] = precede(yshock[4])
+        yshock[5] = follow(yshock[1])
+
+    def y_states():
+        for k in range(4):
+            near_by = k
+            flatten = 1.0 - jnp.maximum(
+                jnp.maximum(yshock[near_by], yshock[near_by + 1]), yshock[near_by + 2]
+            )
+            for f in range(5):
+                lower, upper = edge_states(
+                    prim[f, 2 + k, inside],
+                    yfar[f, k],
+                    ynear[f, k],
+                    flatten,
+                )
+                ylow[f, k] = lower
+                yhigh[f, k] = upper
+
+    def state_ends():
+        for f in range(5):
+            ylow[f, 4] = follow(ylow[f, 0])
+
+    def y_solves():
+        for k in range(4):
+            left = [yhigh[f, k] for f in range(5)]
+            right = [ylow[f, 1 + k] for f in range(5)]
+            values = riemann(left, right, 2)
+            for f in range(5):
+                yflux[f, 1 + k] = values[f]
+
+    def flux_ends():
+        for f in range(5):
+            yflux[f, 0] = precede(yflux[f, 4])
+
+    def turn_out(chosen):
+        for f in range(5):
+            total = []
+            for k in range(4):
+                start = k * PAD
+                across = zflux[f, pl.ds(start + 8, BZC)] - zflux[f, pl.ds(start + 7, BZC)]
+                total.append(across + (yflux[f, 1 + k] - yflux[f, k]))
+            swapped = jnp.concatenate(total, axis=0).T
+            for k in range(COLS):
+                box, lanes = tile_of(k)
+                out_ref[box, f, chosen, lanes] = swapped[lane_rows * k : lane_rows * (k + 1)]
+
+    def steps(chosen):
+        turn_in(chosen)
+        z_faces()
+        prim_ends()
+        y_faces()
+        face_ends()
+        z_states()
+        y_states()
+        state_ends()
+        y_solves()
+        flux_ends()
+        z_solves()
+        turn_out(chosen)
+
+    def turn(index, _):
+        strip(index)
         return 0
 
-    lax.fori_loop(0, COLS // joined, turn_in, 0)
-
-    def y_faces(tile):
-        for f in range(5):
-            get = lambda t, f=f: prim[f, t]
-            here = get(tile)
-            behind = y_back(get, tile, 1)
-            ahead = y_ahead(get, tile, 1)
-            second = y_ahead(get, tile, 2)
-            near[f, tile], far[f, tile] = face_parts(behind, here, ahead, second)
-            if f == 2:
-                vel_m, vel_p = behind, ahead
-            if f == 4:
-                shock[tile] = shock_of(
-                    y_back(get, tile, 2), behind, ahead, second, vel_m, vel_p
-                )
-
-    def z_faces(tile):
-        start = tile * PAD
-        for f in range(5):
-            here = zprim[f, pl.ds(start + 8, BZC)]
-            behind = zprim[f, pl.ds(start + 7, BZC)]
-            ahead = zprim[f, pl.ds(start + 9, BZC)]
-            second = zprim[f, pl.ds(start + 10, BZC)]
-            rise, rest = face_parts(behind, here, ahead, second)
-            znear[f, pl.ds(start + 8, BZC)] = rise
-            zfar[f, pl.ds(start + 8, BZC)] = rest
-            zfar[f, pl.ds(start + 7, 1)] = rest[BZC - 1 :]
-            if f == 3:
-                vel_m, vel_p = behind, ahead
-            if f == 4:
-                level = shock_of(
-                    zprim[f, pl.ds(start + 6, BZC)], behind, ahead, second, vel_m, vel_p
-                )
-                zshock[pl.ds(start + 8, BZC)] = level
-                zshock[pl.ds(start + 7, 1)] = level[BZC - 1 :]
-                zshock[pl.ds(start + 40, 1)] = level[:1]
-
-    def both(y_step, z_step):
-        def turn(index, _):
-            for k in range(ratio):
-                y_step(index * ratio + k)
-            z_step(index)
-            return 0
-
-        lax.fori_loop(0, COLS // ratio, turn, 0)
-
-    both(y_faces, z_faces)
-
-    def y_states(tile):
-        get = lambda t: shock[t]
-        flatten = 1.0 - jnp.maximum(
-            jnp.maximum(y_back(get, tile, 1), shock[tile]), y_ahead(get, tile, 1)
-        )
-        for f in range(5):
-            below = y_back(lambda t, f=f: far[f, t], tile, 1)
-            low[f, tile], high[f, tile] = edge_states(prim[f, tile], below, near[f, tile], flatten)
-
-    def z_states(tile):
-        start = tile * PAD
-        flatten = 1.0 - jnp.maximum(
-            jnp.maximum(zshock[pl.ds(start + 7, BZC)], zshock[pl.ds(start + 8, BZC)]),
-            zshock[pl.ds(start + 9, BZC)],
-        )
-        for f in range(5):
-            lower, upper = edge_states(
-                zprim[f, pl.ds(start + 8, BZC)],
-                zfar[f, pl.ds(start + 7, BZC)],
-                znear[f, pl.ds(start + 8, BZC)],
-                flatten,
-            )
-            zlow[f, pl.ds(start + 8, BZC)] = lower
-            zlow[f, pl.ds(start + 40, 1)] = lower[:1]
-            zhigh[f, pl.ds(start + 8, BZC)] = upper
-
-    both(y_states, z_states)
-
-    def y_flux(tile):
-        left = [high[f, tile] for f in range(5)]
-        right = [y_ahead(lambda t, f=f: low[f, t], tile, 1) for f in range(5)]
-        values = riemann(left, right, 2)
-        for f in range(5):
-            flux[f, tile] = values[f]
-
-    def z_flux(tile):
-        start = tile * PAD
-        left = [zhigh[f, pl.ds(start + 8, BZC)] for f in range(5)]
-        right = [zlow[f, pl.ds(start + 9, BZC)] for f in range(5)]
-        values = riemann(left, right, 3)
-        for f in range(5):
-            zflux[f, pl.ds(start + 8, BZC)] = values[f]
-            zflux[f, pl.ds(start + 7, 1)] = values[f][BZC - 1 :]
-
-    both(y_flux, z_flux)
-
-    def turn_out(quad, _):
-        for f in range(5):
-            across = []
-            for k in range(4):
-                start = (quad * 4 + k) * PAD
-                across.append(zflux[f, pl.ds(start + 8, BZC)] - zflux[f, pl.ds(start + 7, BZC)])
-            turned = jnp.concatenate(across, axis=0).T
-            for k in range(joined):
-                tile = quad * joined + k
-                box, part = tile // TILES, tile % TILES
-                lanes = pl.ds(pl.multiple_of(part * 128, 128), 128)
-                along = flux[f, tile] - y_back(lambda t, f=f: flux[f, t], tile, 1)
-                out_ref[box, f, :, lanes] = along + turned[rows * k : rows * (k + 1)]
-        return 0
-
-    lax.fori_loop(0, COLS // joined, turn_out, 0)
+    lax.fori_loop(0, rows // lane_rows, turn, 0)
 
 
 def whole(refs, box, field, lanes):
@@ -359,8 +384,6 @@
             end_high[f, pl.ds(tile, 1)] = high[f, pl.ds(start + 35, 1)]
             end_low[f, pl.ds(tile, 1)] = low[f, pl.ds(start + 36, 1)]
 
-    columns(faces)
-
     def solve(tile):
         start = tile * PAD
         left = [high[f, pl.ds(start + 3, XC)] for f in range(5)]
@@ -369,7 +392,11 @@
         for f in range(5):
             flux[f, pl.ds(start + 3, XC)] = values[f]
 
-    columns(solve, 2)
+    def faces_and_solve(tile):
+        faces(tile)
+        solve(tile)
+
+    columns(faces_and_solve, 4)
     values = riemann([end_high[f] for f in range(5)], [end_low[f] for f in range(5)], 1)
     for f in range(5):
         end_flux[f] = values[f]
@@ -387,7 +414,7 @@
                 value = 0.5 * (whole(base, box, f, lanes) + value)
             out_ref[box, f, :, lanes] = value
 
-    columns(update)
+    columns(update, 4)
 
 
 VMEM = pl.BlockSpec(memory_space=pltpu.VMEM)
@@ -412,18 +439,21 @@
 
 def plane_sweeps(state):
     rows = state.shape[2]
-    depth = COLS * rows // XC * PAD
-    five = pltpu.VMEM((5, COLS, rows, 128), F32)
-    one = pltpu.VMEM((COLS, rows, 128), F32)
-    five_z = pltpu.VMEM((5, depth, 128), F32)
-    one_z = pltpu.VMEM((depth, 128), F32)
+
+    def fields(*shape):
+        return pltpu.VMEM((5,) + shape + (128,), F32)
+
+    columns_y = [fields(n, BZC) for n in (4, 5, 5, 4, 5)]
+    rows_z = [fields(4 * PAD) for _ in range(5)]
+    scratch = [fields(8, PAD)] + columns_y[:2]
+    scratch += [pltpu.VMEM((6, BZC, 128), F32)] + columns_y[2:]
+    scratch += rows_z[:2] + [pltpu.VMEM((4 * PAD, 128), F32)] + rows_z[2:]
     return pl.pallas_call(
         functools.partial(plane_kernel, rows),
         out_shape=jax.ShapeDtypeStruct(state.shape, F32),
         in_specs=[VMEM],
         out_specs=VMEM,
-        scratch_shapes=[five, five, five, one, five, five, five]
-        + [five_z, five_z, five_z, one_z, five_z, five_z, five_z],
+        scratch_shapes=scratch,
         compiler_params=params(),
         cost_estimate=pl.CostEstimate(
             flops=2_000_000 * rows, bytes_accessed=90_000 * rows, transcendentals=0

time: 142 us -> 130 us (0.915)
  Pallas kernels: 39.1 us -> 27.1 us
    pallas_call x4, Pallas kernels: 24.7 us -> 14.4 us  [plane_sweeps(): pl.pallas_call(functools.partial(plane_kernel, rows), out_shape=jax.Shape...]
    pallas_call x2, Pallas kernels: 13.7 us -> 12 us  [line_sweep(): pl.pallas_call(functools.partial(line_kernel, (len(state), len(plane), le...]
  transfers between devices with their start and end apart: 11 -> 11, of which waited for: 1 -> 1; matrix products, arithmetic and copies ran while one was open for 3% -> 3% of each run, Pallas kernels for 18% -> 11%
where the time goes in v4:
time: 130 us; the launch traced here: 129 us
  starting transfers between devices  70.7 us (54%)
  Pallas kernels  27.1 us (21%)
  blocking collectives  24.3 us (19%)
  local copies, waits for them, and re-layouts  2.99 us (2%)
  other arithmetic  2.18 us (2%)
  between operations  1.63 us (1%)
    ppermute x5, starting transfers between devices, turned(): lax.ppermute(value, 'box', [(i, (i + levels * LEVEL) % count) for i in ra...  37.4 us
    all_gather x1, blocking collectives, level_max(): lax.all_gather(value, 'box', axis_index_groups=level)  24.3 us
    ppermute x4, starting transfers between devices, shifted(): lax.ppermute(value, 'box', [(s, s + steps) for s in range(first, last)])  19.7 us
    pallas_call x4, Pallas kernels, plane_sweeps(): pl.pallas_call(functools.partial(plane_kernel, rows), out_shape=jax.Shape...  14.4 us
    pallas_call x2, Pallas kernels, line_sweep(): pl.pallas_call(functools.partial(line_kernel, (len(state), len(plane), le...  12 us
    ppermute x1, starting transfers between devices, body(): most = lax.ppermute(out_most, 'box', across)  8.84 us
    ppermute x1, starting transfers between devices, body(): last = lax.ppermute(out_last, 'box', across)  4.65 us
  transfers between devices with their start and end apart: 11, of which 1 were waited for; matrix products, arithmetic and copies ran while one was open for 3% of the time, Pallas kernels for 11%

profile of v4, /device:TPU:191, one launch (start us, length us, event | category | flops | bytes accessed | tf_op | source)
XLA Modules:
  0.0 129.3 jit_solution(10271686558272911290)
XLA Ops:
  0.0 0.0 copy-start
  0.0 1.3 %copy-done = f32[2,5,32,1024]{3,2,1,0:T(8,128)S(1)} copy-done((f32[2,5,32,1024]{3,2,1,0:T(8,128)S(1)}, f32[2,5,32,1024]{3,2,1,0:T(8,128)}, u32[]{:S(2)}) %copy-start) | copy-done | bytes 1310744
  1.3 0.0 copy-start.1
  1.3 0.6 fastest.1
  2.0 3.5 %collective-permute-start = (f32[8,128]{1,0:T(8,128)S(1)}, f32[8,128]{1,0:T(8,128)S(1)}, u32[]{:S(2)}, u32[]{:S(2)}) collective-permute-start(f32[8,128]{1,0:T(8,128)S(1)} %fastest.1), channel_id=1, source_target_pairs={{0,32},{1,33},{2,34},{3,35},{4,36},{5,37},{6,38},{7,39},{8,40},{9,... | collective-permute-start | bytes 12296 | tf_op jit(solution)/shard_map/ppermute | solution.py:500
  6.2 0.0 copy-done.1
  6.2 0.0 copy-start.2
  6.2 0.1 dynamic-slice_bitcast_fusion
  6.3 0.7 fusion.2
  7.0 0.0 copy-done.2
  7.0 0.1 compare_convert_fusion.1
  7.1 0.1 add_clamp_fusion.1
  7.2 0.0 collective-permute-done
  7.2 8.8 %collective-permute-start.1 = (f32[5,24,1024]{2,1,0:T(8,128)S(1)}, f32[5,24,1024]{2,1,0:T(8,128)S(1)}, u32[]{:S(2)}, u32[]{:S(2)}) collective-permute-start(f32[5,24,1024]{2,1,0:T(8,128)S(1)} %pad_maximum_fusion), channel_id=1, source_target_pairs={{0,256},{1,257},{2,258},{3,259},{4,260},{5,261},{6,262},{7,263},{8... | collective-permute-start | bytes 1474568 | tf_op jit(solution)/shard_map/ppermute | solution.py:522
  16.0 0.1 pad_add_fusion.slot_ref
  16.1 24.3 %all-gather = f32[256,128]{1,0:T(8,128)S(1)} all-gather(f32[8,128]{1,0:T(8,128)S(1)} %max.24), channel_id=2, replica_groups={{0,1,2,3,4,5,6,7,8,9,10,11,12,13,14,15,16,17,18,19,20,21,22,23,24,25,26..., dimensions={0}, use_global_device_ids=true | all-gather | bytes 135168 | tf_op jit(solution)/shard_map/all_gather | solution.py:495
  40.4 1.9 %collective-permute-start.4 = (f32[8,128]{1,0:T(8,128)S(1)}, f32[8,128]{1,0:T(8,128)S(1)}, u32[]{:S(2)}, u32[]{:S(2)}) collective-permute-start(f32[8,128]{1,0:T(8,128)S(1)} %bitcast_reduce_fusion), channel_id=1, source_target_pairs={{0,192},{1,193},{2,194},{3,195},{4,196},{5,197},{6,198},{7,199},{8... | collective-permute-start | bytes 12296 | tf_op jit(solution)/shard_map/ppermute | solution.py:500
  42.3 8.5 %collective-permute-start.3 = (f32[8,128]{1,0:T(8,128)S(1)}, f32[8,128]{1,0:T(8,128)S(1)}, u32[]{:S(2)}, u32[]{:S(2)}) collective-permute-start(f32[8,128]{1,0:T(8,128)S(1)} %bitcast_reduce_fusion), channel_id=1, source_target_pairs={{0,128},{1,129},{2,130},{3,131},{4,132},{5,133},{6,134},{7,135},{8... | collective-permute-start | bytes 12296 | tf_op jit(solution)/shard_map/ppermute | solution.py:500
  50.8 4.0 %collective-permute-start.2 = (f32[8,128]{1,0:T(8,128)S(1)}, f32[8,128]{1,0:T(8,128)S(1)}, u32[]{:S(2)}, u32[]{:S(2)}) collective-permute-start(f32[8,128]{1,0:T(8,128)S(1)} %bitcast_reduce_fusion), channel_id=1, source_target_pairs={{0,64},{1,65},{2,66},{3,67},{4,68},{5,69},{6,70},{7,71},{8,72},{9,... | collective-permute-start | bytes 12296 | tf_op jit(solution)/shard_map/ppermute | solution.py:500
  54.8 4.7 %collective-permute-start.8 = (f32[5,8,1024]{2,1,0:T(8,128)}, f32[5,8,1024]{2,1,0:T(8,128)}, u32[]{:S(2)}, u32[]{:S(2)}) collective-permute-start(f32[5,8,1024]{2,1,0:T(8,128)} %get-tuple-element.17), channel_id=1, source_target_pairs={{0,256},{1,257},{2,258},{3,259},{4,260},{5,261},{6,262},{7,263},{8... | collective-permute-start | bytes 491528 | tf_op jit(solution)/shard_map/ppermute | solution.py:523
  59.5 0.0 collective-permute-done.4
  59.5 0.0 collective-permute-done.3
  59.5 0.5 collective-permute-done.2
  60.0 19.5 %collective-permute-start.5 = (f32[8,128]{1,0:T(8,128)S(1)}, f32[8,128]{1,0:T(8,128)S(1)}, u32[]{:S(2)}, u32[]{:S(2)}) collective-permute-start(f32[8,128]{1,0:T(8,128)S(1)} %maximum_maximum_fusion), channel_id=1, source_target_pairs={{0,256},{1,257},{2,258},{3,259},{4,260},{5,261},{6,262},{7,263},{8... | collective-permute-start | bytes 12296 | tf_op jit(solution)/shard_map/ppermute | solution.py:500
  79.6 0.0 collective-permute-done.1
  79.6 0.1 slice_select_fusion.1
  79.7 0.1 maximum_select_fusion.state_ref.refs_0_.refs_2_
  79.9 0.8 fusion.1
  80.7 2.5 %collective-permute-start.7 = (f32[2,5,4,1024]{3,2,1,0:T(4,128)}, f32[2,5,4,1024]{3,2,1,0:T(4,128)S(1)}, u32[]{:S(2)}, u32[]{:S(2)}) collective-permute-start(f32[2,5,4,1024]{3,2,1,0:T(4,128)} %get-tuple-element.26), channel_id=1, source_target_pairs={{1,0},{2,1},{3,2},{4,3},{5,4},{6,5},{7,6},{8,7},{9,8},{10,9},{11,1... | collective-permute-start | bytes 491528 | tf_op jit(solution)/shard_map/ppermute | solution.py:488
  83.2 7.3 %collective-permute-start.6 = (f32[2,5,4,1024]{3,2,1,0:T(4,128)}, f32[2,5,4,1024]{3,2,1,0:T(4,128)}, u32[]{:S(2)}, u32[]{:S(2)}) collective-permute-start(f32[2,5,4,1024]{3,2,1,0:T(4,128)} %get-tuple-element.27), channel_id=1, source_target_pairs={{0,1},{1,2},{2,3},{3,4},{4,5},{5,6},{6,7},{7,8},{8,9},{9,10},{10,1... | collective-permute-start | bytes 491528 | tf_op jit(solution)/shard_map/ppermute | solution.py:488
  90.5 1.8 %plane.5.refs_4_ = f32[2,5,8,1024]{3,2,1,0:T(8,128)S(1)} custom-call(f32[2,5,8,1024]{3,2,1,0:T(8,128)S(1)} %get-tuple-element.23.state_ref.refs_1_.refs_3_), custom_call_target="tpu_custom_call" | custom-call | flops 16000000 | bytes 720000 | tf_op jit(solution)/shard_map/plane/pallas_call | solution.py:451
  92.3 3.6 %plane.4.refs_3_ = f32[2,5,16,1024]{3,2,1,0:T(8,128)S(1)} custom-call(f32[2,5,16,1024]{3,2,1,0:T(8,128)S(1)} %maximum_select_fusion.state_ref.refs_0_.refs_2_), custom_call_target="tpu_custom_call" | custom-call | flops 32000000 | bytes 1440000 | tf_op jit(solution)/shard_map/plane/pallas_call | solution.py:451
  95.9 0.0 collective-permute-done.8
  95.9 0.0 collective-permute-done.5
  95.9 0.6 maximum_reduce_fusion
  97.2 1.0 slice_select_fusion.state_ref.refs_2_.refs_4_
  98.2 1.8 %plane.6.refs_5_ = f32[2,5,8,1024]{3,2,1,0:T(8,128)S(1)} custom-call(f32[2,5,8,1024]{3,2,1,0:T(8,128)S(1)} %slice_select_fusion.state_ref.refs_2_.refs_4_), custom_call_target="tpu_custom_call" | custom-call | flops 16000000 | bytes 720000 | tf_op jit(solution)/shard_map/plane/pallas_call | solution.py:451
  100.0 0.0 collective-permute-done.7.above_ref
  100.0 0.0 collective-permute-done.6.below_ref
  100.0 5.6 %line.2.state_ref.refs_0_ = f32[2,5,32,1024]{3,2,1,0:T(8,128)S(1)} custom-call(s32[2,4]{1,0:T(2,128)S(1)} %pad_add_fusion.slot_ref, f32[1]{0:T(128)} %bitcast.3.ratio_ref, f32[2,5,4,1024]{3,2,1,0:T(4,128)} %collective-permute-done.6.below_ref, f32[2,5,4,1024]{3,2,1,0:T(4,128)S(1)} %collective-permute-done.7.above_ref, ...), custom_call_target="tpu_custom_call" | custom-call | flops 30000000 | bytes 4000000 | tf_op jit(solution)/shard_map/line/pallas_call | solution.py:471
  105.6 0.1 fusion
  105.7 1.9 %collective-permute-start.10 = (f32[2,5,4,1024]{3,2,1,0:T(4,128)S(1)}, f32[2,5,4,1024]{3,2,1,0:T(4,128)S(1)}, u32[]{:S(2)}, u32[]{:S(2)}) collective-permute-start(f32[2,5,4,1024]{3,2,1,0:T(4,128)S(1)} %get-tuple-element.21), channel_id=1, source_target_pairs={{1,0},{2,1},{3,2},{4,3},{5,4},{6,5},{7,6},{8,7},{9,8},{10,9},{11,1... | collective-permute-start | bytes 491528 | tf_op jit(solution)/shard_map/ppermute | solution.py:488
  107.6 8.0 %collective-permute-start.9 = (f32[2,5,4,1024]{3,2,1,0:T(4,128)S(1)}, f32[2,5,4,1024]{3,2,1,0:T(4,128)S(1)}, u32[]{:S(2)}, u32[]{:S(2)}) collective-permute-start(f32[2,5,4,1024]{3,2,1,0:T(4,128)S(1)} %get-tuple-element.22), channel_id=1, source_target_pairs={{0,1},{1,2},{2,3},{3,4},{4,5},{5,6},{6,7},{7,8},{8,9},{9,10},{10,1... | collective-permute-start | bytes 491528 | tf_op jit(solution)/shard_map/ppermute | solution.py:488
  115.6 7.2 %plane.7.refs_1_ = f32[2,5,32,1024]{3,2,1,0:T(8,128)S(1)} custom-call(f32[2,5,32,1024]{3,2,1,0:T(8,128)S(1)} %line.2.state_ref.refs_0_), custom_call_target="tpu_custom_call" | custom-call | flops 64000000 | bytes 2880000 | tf_op jit(solution)/shard_map/plane/pallas_call | solution.py:451
  122.9 0.0 collective-permute-done.10.above_ref
  122.9 0.0 collective-permute-done.9.below_ref
  122.9 6.4 %line.3 = f32[2,5,32,1024]{3,2,1,0:T(8,128)} custom-call(s32[2,4]{1,0:T(2,128)S(1)} %pad_add_fusion.slot_ref, f32[1]{0:T(128)} %bitcast.3.ratio_ref, f32[2,5,4,1024]{3,2,1,0:T(4,128)S(1)} %collective-permute-done.9.below_ref, f32[2,5,4,1024]{3,2,1,0:T(4,128)S(1)} %collective-permute-done.10.above_ref, f32[2,5,32,1024]{3,2,1,0:T(8,128)S(1)} %line.2.state_ref.refs_0_, ...), custom_call_target="tpu_custom_call" | custom-call | flops 30000000 | bytes 4000000 | tf_op jit(solution)/shard_map/line/pallas_call | solution.py:471
  (8 shorter events, 0.2 us)
Async XLA Ops:
  0.0 1.3 %copy-start = (f32[2,5,32,1024]{3,2,1,0:T(8,128)S(1)}, f32[2,5,32,1024]{3,2,1,0:T(8,128)}, u32[]{:S(2)}) copy-start(f32[2,5,32,1024]{3,2,1,0:T(8,128)} %state_ref.1) | copy-start | bytes 3932164
  1.3 4.9 %copy-start.1 = (f32[2,5,32,1024]{3,2,1,0:T(8,128)S(1)}, f32[2,5,32,1024]{3,2,1,0:T(8,128)}, u32[]{:S(2)}) copy-start(f32[2,5,32,1024]{3,2,1,0:T(8,128)} %state_ref.1) | copy-start | bytes 3932164
  2.0 5.2 %collective-permute-start = (f32[8,128]{1,0:T(8,128)S(1)}, f32[8,128]{1,0:T(8,128)S(1)}, u32[]{:S(2)}, u32[]{:S(2)}) collective-permute-start(f32[8,128]{1,0:T(8,128)S(1)} %fastest.1), channel_id=1, source_target_pairs={{0,32},{1,33},{2,34},{3,35},{4,36},{5,37},{6,38},{7,39},{8,40},{9,... | collective-permute-start | bytes 12296 | tf_op jit(solution)/shard_map/ppermute | solution.py:500
  6.2 0.8 copy-start.2
  7.2 72.4 %collective-permute-start.1 = (f32[5,24,1024]{2,1,0:T(8,128)S(1)}, f32[5,24,1024]{2,1,0:T(8,128)S(1)}, u32[]{:S(2)}, u32[]{:S(2)}) collective-permute-start(f32[5,24,1024]{2,1,0:T(8,128)S(1)} %pad_maximum_fusion), channel_id=1, source_target_pairs={{0,256},{1,257},{2,258},{3,259},{4,260},{5,261},{6,262},{7,263},{8... | collective-permute-start | bytes 1474568 | tf_op jit(solution)/shard_map/ppermute | solution.py:522
  40.4 19.1 %collective-permute-start.4 = (f32[8,128]{1,0:T(8,128)S(1)}, f32[8,128]{1,0:T(8,128)S(1)}, u32[]{:S(2)}, u32[]{:S(2)}) collective-permute-start(f32[8,128]{1,0:T(8,128)S(1)} %bitcast_reduce_fusion), channel_id=1, source_target_pairs={{0,192},{1,193},{2,194},{3,195},{4,196},{5,197},{6,198},{7,199},{8... | collective-permute-start | bytes 12296 | tf_op jit(solution)/shard_map/ppermute | solution.py:500
  42.3 17.1 %collective-permute-start.3 = (f32[8,128]{1,0:T(8,128)S(1)}, f32[8,128]{1,0:T(8,128)S(1)}, u32[]{:S(2)}, u32[]{:S(2)}) collective-permute-start(f32[8,128]{1,0:T(8,128)S(1)} %bitcast_reduce_fusion), channel_id=1, source_target_pairs={{0,128},{1,129},{2,130},{3,131},{4,132},{5,133},{6,134},{7,135},{8... | collective-permute-start | bytes 12296 | tf_op jit(solution)/shard_map/ppermute | solution.py:500
  50.8 9.2 %collective-permute-start.2 = (f32[8,128]{1,0:T(8,128)S(1)}, f32[8,128]{1,0:T(8,128)S(1)}, u32[]{:S(2)}, u32[]{:S(2)}) collective-permute-start(f32[8,128]{1,0:T(8,128)S(1)} %bitcast_reduce_fusion), channel_id=1, source_target_pairs={{0,64},{1,65},{2,66},{3,67},{4,68},{5,69},{6,70},{7,71},{8,72},{9,... | collective-permute-start | bytes 12296 | tf_op jit(solution)/shard_map/ppermute | solution.py:500
  54.8 41.1 %collective-permute-start.8 = (f32[5,8,1024]{2,1,0:T(8,128)}, f32[5,8,1024]{2,1,0:T(8,128)}, u32[]{:S(2)}, u32[]{:S(2)}) collective-permute-start(f32[5,8,1024]{2,1,0:T(8,128)} %get-tuple-element.17), channel_id=1, source_target_pairs={{0,256},{1,257},{2,258},{3,259},{4,260},{5,261},{6,262},{7,263},{8... | collective-permute-start | bytes 491528 | tf_op jit(solution)/shard_map/ppermute | solution.py:523
  60.0 35.9 %collective-permute-start.5 = (f32[8,128]{1,0:T(8,128)S(1)}, f32[8,128]{1,0:T(8,128)S(1)}, u32[]{:S(2)}, u32[]{:S(2)}) collective-permute-start(f32[8,128]{1,0:T(8,128)S(1)} %maximum_maximum_fusion), channel_id=1, source_target_pairs={{0,256},{1,257},{2,258},{3,259},{4,260},{5,261},{6,262},{7,263},{8... | collective-permute-start | bytes 12296 | tf_op jit(solution)/shard_map/ppermute | solution.py:500
  80.7 19.3 %collective-permute-start.7 = (f32[2,5,4,1024]{3,2,1,0:T(4,128)}, f32[2,5,4,1024]{3,2,1,0:T(4,128)S(1)}, u32[]{:S(2)}, u32[]{:S(2)}) collective-permute-start(f32[2,5,4,1024]{3,2,1,0:T(4,128)} %get-tuple-element.26), channel_id=1, source_target_pairs={{1,0},{2,1},{3,2},{4,3},{5,4},{6,5},{7,6},{8,7},{9,8},{10,9},{11,1... | collective-permute-start | bytes 491528 | tf_op jit(solution)/shard_map/ppermute | solution.py:488
  83.2 16.9 %collective-permute-start.6 = (f32[2,5,4,1024]{3,2,1,0:T(4,128)}, f32[2,5,4,1024]{3,2,1,0:T(4,128)}, u32[]{:S(2)}, u32[]{:S(2)}) collective-permute-start(f32[2,5,4,1024]{3,2,1,0:T(4,128)} %get-tuple-element.27), channel_id=1, source_target_pairs={{0,1},{1,2},{2,3},{3,4},{4,5},{5,6},{6,7},{7,8},{8,9},{9,10},{10,1... | collective-permute-start | bytes 491528 | tf_op jit(solution)/shard_map/ppermute | solution.py:488
  105.7 17.2 %collective-permute-start.10 = (f32[2,5,4,1024]{3,2,1,0:T(4,128)S(1)}, f32[2,5,4,1024]{3,2,1,0:T(4,128)S(1)}, u32[]{:S(2)}, u32[]{:S(2)}) collective-permute-start(f32[2,5,4,1024]{3,2,1,0:T(4,128)S(1)} %get-tuple-element.21), channel_id=1, source_target_pairs={{1,0},{2,1},{3,2},{4,3},{5,4},{6,5},{7,6},{8,7},{9,8},{10,9},{11,1... | collective-permute-start | bytes 491528 | tf_op jit(solution)/shard_map/ppermute | solution.py:488
  107.6 15.3 %collective-permute-start.9 = (f32[2,5,4,1024]{3,2,1,0:T(4,128)S(1)}, f32[2,5,4,1024]{3,2,1,0:T(4,128)S(1)}, u32[]{:S(2)}, u32[]{:S(2)}) collective-permute-start(f32[2,5,4,1024]{3,2,1,0:T(4,128)S(1)} %get-tuple-element.22), channel_id=1, source_target_pairs={{0,1},{1,2},{2,3},{3,4},{4,5},{5,6},{6,7},{7,8},{8,9},{9,10},{10,1... | collective-permute-start | bytes 491528 | tf_op jit(solution)/shard_map/ppermute | solution.py:488

commit v5 on v4

--- a/solution.py
+++ b/solution.py
@@ -328,7 +328,7 @@
     )
 
 
-def line_kernel(counts, slot_ref, ratio_ref, below_ref, above_ref, *refs):
+def line_kernel(counts, slot_ref, peak_ref, final_ref, below_ref, above_ref, *refs):
     groups = []
     for n in counts:
         groups.append(refs[:n])
@@ -396,11 +396,12 @@
         faces(tile)
         solve(tile)
 
-    columns(faces_and_solve, 4)
+    columns(faces_and_solve, 8)
     values = riemann([end_high[f] for f in range(5)], [end_low[f] for f in range(5)], 1)
     for f in range(5):
         end_flux[f] = values[f]
-    ratio = ratio_ref[0]
+    largest = jnp.max(jnp.maximum(peak_ref[...], final_ref[...]), axis=(0, 1), keepdims=True)
+    ratio = jnp.broadcast_to(COURANT / largest, (XC, 128))
 
     def update(tile):
         box, part = tile // TILES, tile % TILES
@@ -414,7 +415,7 @@
                 value = 0.5 * (whole(base, box, f, lanes) + value)
             out_ref[box, f, :, lanes] = value
 
-    columns(update, 4)
+    columns(update, 8)
 
 
 VMEM = pl.BlockSpec(memory_space=pltpu.VMEM)
@@ -462,16 +463,16 @@
     )(state)
 
 
-def line_sweep(slots, ratio, below, above, state, plane, base=()):
+def line_sweep(slots, peaks, below, above, state, plane, base=()):
     five = pltpu.VMEM((5, COLS * PAD, 128), F32)
     one = pltpu.VMEM((COLS * PAD, 128), F32)
     end = pltpu.VMEM((5, COLS, 128), F32)
-    args = [slots, ratio, below, above, *state, *plane, *base]
+    args = [slots, *peaks, below, above, *state, *plane, *base]
     shape = (slots.shape[0], 5, XC, TILES * 128)
     return pl.pallas_call(
         functools.partial(line_kernel, (len(state), len(plane), len(base))),
         out_shape=jax.ShapeDtypeStruct(shape, F32),
-        in_specs=[SMEM, SMEM] + [VMEM] * (len(args) - 2),
+        in_specs=[SMEM] + [VMEM] * (len(args) - 1),
         out_specs=VMEM,
         scratch_shapes=[five, five, five, one, five, five, five, end, end, end],
         compiler_params=params(),
@@ -547,12 +548,12 @@
     last, *planes = lax.optimization_barrier((last, *planes))
     third = jnp.where(chosen, last[None], quarters(cell_state, 2))
     planes.append(plane_sweeps(third))
-    ratio = (COURANT / jnp.max(jnp.maximum(peak, final))).reshape(1)
+    peaks = (peak, final)
     after = (outer, second, third)
-    first = line_sweep(table, ratio, below, above, after, planes)
+    first = line_sweep(table, peaks, below, above, after, planes)
     below = shifted(first[:, :, -GHOST:], 1)
     above = shifted(first[:, :, :GHOST], -1)
-    return line_sweep(table, ratio, below, above, (first,), (plane_sweeps(first),), after)
+    return line_sweep(table, peaks, below, above, (first,), (plane_sweeps(first),), after)
 
 
 def solution(mesh):

time: 130 us -> 126 us (0.969)
  other arithmetic: 2.18 us -> 0.66 us
  transfers between devices with their start and end apart: 11 -> 11, of which waited for: 1 -> 1; matrix products, arithmetic and copies ran while one was open for 3% -> 1% of each run, Pallas kernels for 11% -> 12%
where the time goes in v5:
time: 126 us; the launch traced here: 125 us
  starting transfers between devices  70.5 us (56%)
  Pallas kernels  26.4 us (21%)
  blocking collectives  24.3 us (19%)
  local copies, waits for them, and re-layouts  2.13 us (2%)
    ppermute x5, starting transfers between devices, turned(): lax.ppermute(value, 'box', [(i, (i + levels * LEVEL) % count) for i in ra...  37.1 us
    all_gather x1, blocking collectives, level_max(): lax.all_gather(value, 'box', axis_index_groups=level)  24.3 us
    ppermute x4, starting transfers between devices, shifted(): lax.ppermute(value, 'box', [(s, s + steps) for s in range(first, last)])  19.7 us
    pallas_call x4, Pallas kernels, plane_sweeps(): pl.pallas_call(functools.partial(plane_kernel, rows), out_shape=jax.Shape...  14.4 us
    pallas_call x2, Pallas kernels, line_sweep(): pl.pallas_call(functools.partial(line_kernel, (len(state), len(plane), le...  11.3 us
    ppermute x1, starting transfers between devices, body(): most = lax.ppermute(out_most, 'box', across)  8.96 us
    ppermute x1, starting transfers between devices, body(): last = lax.ppermute(out_last, 'box', across)  4.65 us
  transfers between devices with their start and end apart: 11, of which 1 were waited for; matrix products, arithmetic and copies ran while one was open for 1% of the time, Pallas kernels for 12%

profile of v5, /device:TPU:191, one launch (start us, length us, event | category | flops | bytes accessed | tf_op | source)
XLA Modules:
  0.0 125.4 jit_solution(15729004146569441904)
XLA Ops:
  0.0 0.0 copy-start
  0.0 1.3 %copy-done = f32[2,5,32,1024]{3,2,1,0:T(8,128)S(1)} copy-done((f32[2,5,32,1024]{3,2,1,0:T(8,128)S(1)}, f32[2,5,32,1024]{3,2,1,0:T(8,128)}, u32[]{:S(2)}) %copy-start) | copy-done | bytes 1310744
  1.3 0.0 copy-start.1
  1.3 0.6 fastest.1
  2.0 3.5 %collective-permute-start = (f32[8,128]{1,0:T(8,128)S(1)}, f32[8,128]{1,0:T(8,128)S(1)}, u32[]{:S(2)}, u32[]{:S(2)}) collective-permute-start(f32[8,128]{1,0:T(8,128)S(1)} %fastest.1), channel_id=1, source_target_pairs={{0,32},{1,33},{2,34},{3,35},{4,36},{5,37},{6,38},{7,39},{8,40},{9,... | collective-permute-start | bytes 12296 | tf_op jit(solution)/shard_map/ppermute | solution.py:501
  6.2 0.0 copy-done.1
  6.2 0.0 copy-start.2
  6.2 0.1 dynamic-slice_bitcast_fusion
  6.3 0.5 copy-done.2
  6.9 0.1 compare_convert_fusion.1
  6.9 0.1 add_clamp_fusion.1
  7.1 0.0 collective-permute-done
  7.1 9.0 %collective-permute-start.1 = (f32[5,24,1024]{2,1,0:T(8,128)S(1)}, f32[5,24,1024]{2,1,0:T(8,128)S(1)}, u32[]{:S(2)}, u32[]{:S(2)}) collective-permute-start(f32[5,24,1024]{2,1,0:T(8,128)S(1)} %pad_maximum_fusion), channel_id=1, source_target_pairs={{0,256},{1,257},{2,258},{3,259},{4,260},{5,261},{6,262},{7,263},{8... | collective-permute-start | bytes 1474568 | tf_op jit(solution)/shard_map/ppermute | solution.py:523
  16.0 0.1 pad_add_fusion.slot_ref
  16.1 24.3 %all-gather = f32[256,128]{1,0:T(8,128)S(1)} all-gather(f32[8,128]{1,0:T(8,128)S(1)} %max.21), channel_id=2, replica_groups={{0,1,2,3,4,5,6,7,8,9,10,11,12,13,14,15,16,17,18,19,20,21,22,23,24,25,26..., dimensions={0}, use_global_device_ids=true | all-gather | bytes 135168 | tf_op jit(solution)/shard_map/all_gather | solution.py:496
  40.4 1.9 %collective-permute-start.4 = (f32[8,128]{1,0:T(8,128)S(1)}, f32[8,128]{1,0:T(8,128)S(1)}, u32[]{:S(2)}, u32[]{:S(2)}) collective-permute-start(f32[8,128]{1,0:T(8,128)S(1)} %bitcast_reduce_fusion), channel_id=1, source_target_pairs={{0,192},{1,193},{2,194},{3,195},{4,196},{5,197},{6,198},{7,199},{8... | collective-permute-start | bytes 12296 | tf_op jit(solution)/shard_map/ppermute | solution.py:501
  42.3 8.4 %collective-permute-start.3 = (f32[8,128]{1,0:T(8,128)S(1)}, f32[8,128]{1,0:T(8,128)S(1)}, u32[]{:S(2)}, u32[]{:S(2)}) collective-permute-start(f32[8,128]{1,0:T(8,128)S(1)} %bitcast_reduce_fusion), channel_id=1, source_target_pairs={{0,128},{1,129},{2,130},{3,131},{4,132},{5,133},{6,134},{7,135},{8... | collective-permute-start | bytes 12296 | tf_op jit(solution)/shard_map/ppermute | solution.py:501
  50.7 4.1 %collective-permute-start.2 = (f32[8,128]{1,0:T(8,128)S(1)}, f32[8,128]{1,0:T(8,128)S(1)}, u32[]{:S(2)}, u32[]{:S(2)}) collective-permute-start(f32[8,128]{1,0:T(8,128)S(1)} %bitcast_reduce_fusion), channel_id=1, source_target_pairs={{0,64},{1,65},{2,66},{3,67},{4,68},{5,69},{6,70},{7,71},{8,72},{9,... | collective-permute-start | bytes 12296 | tf_op jit(solution)/shard_map/ppermute | solution.py:501
  54.8 4.6 %collective-permute-start.8 = (f32[5,8,1024]{2,1,0:T(8,128)S(1)}, f32[5,8,1024]{2,1,0:T(8,128)S(1)}, u32[]{:S(2)}, u32[]{:S(2)}) collective-permute-start(f32[5,8,1024]{2,1,0:T(8,128)S(1)} %get-tuple-element.17), channel_id=1, source_target_pairs={{0,256},{1,257},{2,258},{3,259},{4,260},{5,261},{6,262},{7,263},{8... | collective-permute-start | bytes 491528 | tf_op jit(solution)/shard_map/ppermute | solution.py:524
  59.5 0.0 collective-permute-done.4
  59.5 0.0 collective-permute-done.3
  59.5 0.5 collective-permute-done.2
  60.0 19.2 %collective-permute-start.5 = (f32[8,128]{1,0:T(8,128)S(1)}, f32[8,128]{1,0:T(8,128)S(1)}, u32[]{:S(2)}, u32[]{:S(2)}) collective-permute-start(f32[8,128]{1,0:T(8,128)S(1)} %maximum_maximum_fusion.peak_ref), channel_id=1, source_target_pairs={{0,256},{1,257},{2,258},{3,259},{4,260},{5,261},{6,262},{7,263},{8... | collective-permute-start | bytes 12296 | tf_op jit(solution)/shard_map/ppermute | solution.py:501
  79.2 0.0 collective-permute-done.1
  79.3 0.1 slice_select_fusion.1
  79.4 0.1 maximum_select_fusion.state_ref.refs_0_.refs_2_
  79.6 0.1 fusion.1
  79.6 2.6 %collective-permute-start.7 = (f32[2,5,4,1024]{3,2,1,0:T(4,128)S(1)}, f32[2,5,4,1024]{3,2,1,0:T(4,128)S(1)}, u32[]{:S(2)}, u32[]{:S(2)}) collective-permute-start(f32[2,5,4,1024]{3,2,1,0:T(4,128)S(1)} %get-tuple-element.26), channel_id=1, source_target_pairs={{1,0},{2,1},{3,2},{4,3},{5,4},{6,5},{7,6},{8,7},{9,8},{10,9},{11,1... | collective-permute-start | bytes 491528 | tf_op jit(solution)/shard_map/ppermute | solution.py:489
  82.2 7.2 %collective-permute-start.6 = (f32[2,5,4,1024]{3,2,1,0:T(4,128)S(1)}, f32[2,5,4,1024]{3,2,1,0:T(4,128)S(1)}, u32[]{:S(2)}, u32[]{:S(2)}) collective-permute-start(f32[2,5,4,1024]{3,2,1,0:T(4,128)S(1)} %get-tuple-element.27), channel_id=1, source_target_pairs={{0,1},{1,2},{2,3},{3,4},{4,5},{5,6},{6,7},{7,8},{8,9},{9,10},{10,1... | collective-permute-start | bytes 491528 | tf_op jit(solution)/shard_map/ppermute | solution.py:489
  89.4 1.8 %plane.5.refs_4_ = f32[2,5,8,1024]{3,2,1,0:T(8,128)S(1)} custom-call(f32[2,5,8,1024]{3,2,1,0:T(8,128)S(1)} %get-tuple-element.23.state_ref.refs_1_.refs_3_), custom_call_target="tpu_custom_call" | custom-call | flops 16000000 | bytes 720000 | tf_op jit(solution)/shard_map/plane/pallas_call | solution.py:452
  91.2 3.6 %plane.4.refs_3_ = f32[2,5,16,1024]{3,2,1,0:T(8,128)S(1)} custom-call(f32[2,5,16,1024]{3,2,1,0:T(8,128)S(1)} %maximum_select_fusion.state_ref.refs_0_.refs_2_), custom_call_target="tpu_custom_call" | custom-call | flops 32000000 | bytes 1440000 | tf_op jit(solution)/shard_map/plane/pallas_call | solution.py:452
  94.8 0.0 collective-permute-done.8
  94.9 0.1 slice_select_fusion.state_ref.refs_2_.refs_4_
  95.0 1.8 %plane.6.refs_5_ = f32[2,5,8,1024]{3,2,1,0:T(8,128)S(1)} custom-call(f32[2,5,8,1024]{3,2,1,0:T(8,128)S(1)} %slice_select_fusion.state_ref.refs_2_.refs_4_), custom_call_target="tpu_custom_call" | custom-call | flops 16000000 | bytes 720000 | tf_op jit(solution)/shard_map/plane/pallas_call | solution.py:452
  96.8 0.0 collective-permute-done.5.final_ref
  96.8 0.0 collective-permute-done.7.above_ref
  96.8 0.0 collective-permute-done.6.below_ref
  96.8 5.0 %line.2.state_ref.refs_0_ = f32[2,5,32,1024]{3,2,1,0:T(8,128)S(1)} custom-call(s32[2,4]{1,0:T(2,128)S(1)} %pad_add_fusion.slot_ref, f32[8,128]{1,0:T(8,128)S(1)} %maximum_maximum_fusion.peak_ref, f32[8,128]{1,0:T(8,128)S(1)} %collective-permute-done.5.final_ref, f32[2,5,4,1024]{3,2,1,0:T(4,128)S(1)} %collective-permute-done.6.below_ref, ...), custom_call_target="tpu_custom_call" | custom-call | flops 30000000 | bytes 4000000 | tf_op jit(solution)/shard_map/line/pallas_call | solution.py:472
  101.8 0.1 fusion
  101.9 1.9 %collective-permute-start.10 = (f32[2,5,4,1024]{3,2,1,0:T(4,128)S(1)}, f32[2,5,4,1024]{3,2,1,0:T(4,128)S(1)}, u32[]{:S(2)}, u32[]{:S(2)}) collective-permute-start(f32[2,5,4,1024]{3,2,1,0:T(4,128)S(1)} %get-tuple-element.21), channel_id=1, source_target_pairs={{1,0},{2,1},{3,2},{4,3},{5,4},{6,5},{7,6},{8,7},{9,8},{10,9},{11,1... | collective-permute-start | bytes 491528 | tf_op jit(solution)/shard_map/ppermute | solution.py:489
  103.8 8.0 %collective-permute-start.9 = (f32[2,5,4,1024]{3,2,1,0:T(4,128)S(1)}, f32[2,5,4,1024]{3,2,1,0:T(4,128)S(1)}, u32[]{:S(2)}, u32[]{:S(2)}) collective-permute-start(f32[2,5,4,1024]{3,2,1,0:T(4,128)S(1)} %get-tuple-element.22), channel_id=1, source_target_pairs={{0,1},{1,2},{2,3},{3,4},{4,5},{5,6},{6,7},{7,8},{8,9},{9,10},{10,1... | collective-permute-start | bytes 491528 | tf_op jit(solution)/shard_map/ppermute | solution.py:489
  111.9 7.2 %plane.7.refs_1_ = f32[2,5,32,1024]{3,2,1,0:T(8,128)S(1)} custom-call(f32[2,5,32,1024]{3,2,1,0:T(8,128)S(1)} %line.2.state_ref.refs_0_), custom_call_target="tpu_custom_call" | custom-call | flops 64000000 | bytes 2880000 | tf_op jit(solution)/shard_map/plane/pallas_call | solution.py:452
  119.1 0.0 collective-permute-done.10.above_ref
  119.1 0.0 collective-permute-done.9.below_ref
  119.1 6.3 %line.3 = f32[2,5,32,1024]{3,2,1,0:T(8,128)} custom-call(s32[2,4]{1,0:T(2,128)S(1)} %pad_add_fusion.slot_ref, f32[8,128]{1,0:T(8,128)S(1)} %maximum_maximum_fusion.peak_ref, f32[8,128]{1,0:T(8,128)S(1)} %collective-permute-done.5.final_ref, f32[2,5,4,1024]{3,2,1,0:T(4,128)S(1)} %collective-permute-done.9.below_ref, ...), custom_call_target="tpu_custom_call" | custom-call | flops 30000000 | bytes 4000000 | tf_op jit(solution)/shard_map/line/pallas_call | solution.py:472
  (9 shorter events, 0.2 us)
Async XLA Ops:
  0.0 1.3 %copy-start = (f32[2,5,32,1024]{3,2,1,0:T(8,128)S(1)}, f32[2,5,32,1024]{3,2,1,0:T(8,128)}, u32[]{:S(2)}) copy-start(f32[2,5,32,1024]{3,2,1,0:T(8,128)} %state_ref.1) | copy-start | bytes 3932164
  1.3 4.9 %copy-start.1 = (f32[2,5,32,1024]{3,2,1,0:T(8,128)S(1)}, f32[2,5,32,1024]{3,2,1,0:T(8,128)}, u32[]{:S(2)}) copy-start(f32[2,5,32,1024]{3,2,1,0:T(8,128)} %state_ref.1) | copy-start | bytes 3932164
  2.0 5.1 %collective-permute-start = (f32[8,128]{1,0:T(8,128)S(1)}, f32[8,128]{1,0:T(8,128)S(1)}, u32[]{:S(2)}, u32[]{:S(2)}) collective-permute-start(f32[8,128]{1,0:T(8,128)S(1)} %fastest.1), channel_id=1, source_target_pairs={{0,32},{1,33},{2,34},{3,35},{4,36},{5,37},{6,38},{7,39},{8,40},{9,... | collective-permute-start | bytes 12296 | tf_op jit(solution)/shard_map/ppermute | solution.py:501
  6.2 0.7 copy-start.2
  7.1 72.2 %collective-permute-start.1 = (f32[5,24,1024]{2,1,0:T(8,128)S(1)}, f32[5,24,1024]{2,1,0:T(8,128)S(1)}, u32[]{:S(2)}, u32[]{:S(2)}) collective-permute-start(f32[5,24,1024]{2,1,0:T(8,128)S(1)} %pad_maximum_fusion), channel_id=1, source_target_pairs={{0,256},{1,257},{2,258},{3,259},{4,260},{5,261},{6,262},{7,263},{8... | collective-permute-start | bytes 1474568 | tf_op jit(solution)/shard_map/ppermute | solution.py:523
  40.4 19.1 %collective-permute-start.4 = (f32[8,128]{1,0:T(8,128)S(1)}, f32[8,128]{1,0:T(8,128)S(1)}, u32[]{:S(2)}, u32[]{:S(2)}) collective-permute-start(f32[8,128]{1,0:T(8,128)S(1)} %bitcast_reduce_fusion), channel_id=1, source_target_pairs={{0,192},{1,193},{2,194},{3,195},{4,196},{5,197},{6,198},{7,199},{8... | collective-permute-start | bytes 12296 | tf_op jit(solution)/shard_map/ppermute | solution.py:501
  42.3 17.1 %collective-permute-start.3 = (f32[8,128]{1,0:T(8,128)S(1)}, f32[8,128]{1,0:T(8,128)S(1)}, u32[]{:S(2)}, u32[]{:S(2)}) collective-permute-start(f32[8,128]{1,0:T(8,128)S(1)} %bitcast_reduce_fusion), channel_id=1, source_target_pairs={{0,128},{1,129},{2,130},{3,131},{4,132},{5,133},{6,134},{7,135},{8... | collective-permute-start | bytes 12296 | tf_op jit(solution)/shard_map/ppermute | solution.py:501
  50.7 9.3 %collective-permute-start.2 = (f32[8,128]{1,0:T(8,128)S(1)}, f32[8,128]{1,0:T(8,128)S(1)}, u32[]{:S(2)}, u32[]{:S(2)}) collective-permute-start(f32[8,128]{1,0:T(8,128)S(1)} %bitcast_reduce_fusion), channel_id=1, source_target_pairs={{0,64},{1,65},{2,66},{3,67},{4,68},{5,69},{6,70},{7,71},{8,72},{9,... | collective-permute-start | bytes 12296 | tf_op jit(solution)/shard_map/ppermute | solution.py:501
  54.8 40.0 %collective-permute-start.8 = (f32[5,8,1024]{2,1,0:T(8,128)S(1)}, f32[5,8,1024]{2,1,0:T(8,128)S(1)}, u32[]{:S(2)}, u32[]{:S(2)}) collective-permute-start(f32[5,8,1024]{2,1,0:T(8,128)S(1)} %get-tuple-element.17), channel_id=1, source_target_pairs={{0,256},{1,257},{2,258},{3,259},{4,260},{5,261},{6,262},{7,263},{8... | collective-permute-start | bytes 491528 | tf_op jit(solution)/shard_map/ppermute | solution.py:524
  60.0 36.7 %collective-permute-start.5 = (f32[8,128]{1,0:T(8,128)S(1)}, f32[8,128]{1,0:T(8,128)S(1)}, u32[]{:S(2)}, u32[]{:S(2)}) collective-permute-start(f32[8,128]{1,0:T(8,128)S(1)} %maximum_maximum_fusion.peak_ref), channel_id=1, source_target_pairs={{0,256},{1,257},{2,258},{3,259},{4,260},{5,261},{6,262},{7,263},{8... | collective-permute-start | bytes 12296 | tf_op jit(solution)/shard_map/ppermute | solution.py:501
  79.6 17.1 %collective-permute-start.7 = (f32[2,5,4,1024]{3,2,1,0:T(4,128)S(1)}, f32[2,5,4,1024]{3,2,1,0:T(4,128)S(1)}, u32[]{:S(2)}, u32[]{:S(2)}) collective-permute-start(f32[2,5,4,1024]{3,2,1,0:T(4,128)S(1)} %get-tuple-element.26), channel_id=1, source_target_pairs={{1,0},{2,1},{3,2},{4,3},{5,4},{6,5},{7,6},{8,7},{9,8},{10,9},{11,1... | collective-permute-start | bytes 491528 | tf_op jit(solution)/shard_map/ppermute | solution.py:489
  82.2 14.5 %collective-permute-start.6 = (f32[2,5,4,1024]{3,2,1,0:T(4,128)S(1)}, f32[2,5,4,1024]{3,2,1,0:T(4,128)S(1)}, u32[]{:S(2)}, u32[]{:S(2)}) collective-permute-start(f32[2,5,4,1024]{3,2,1,0:T(4,128)S(1)} %get-tuple-element.27), channel_id=1, source_target_pairs={{0,1},{1,2},{2,3},{3,4},{4,5},{5,6},{6,7},{7,8},{8,9},{9,10},{10,1... | collective-permute-start | bytes 491528 | tf_op jit(solution)/shard_map/ppermute | solution.py:489
  101.9 17.2 %collective-permute-start.10 = (f32[2,5,4,1024]{3,2,1,0:T(4,128)S(1)}, f32[2,5,4,1024]{3,2,1,0:T(4,128)S(1)}, u32[]{:S(2)}, u32[]{:S(2)}) collective-permute-start(f32[2,5,4,1024]{3,2,1,0:T(4,128)S(1)} %get-tuple-element.21), channel_id=1, source_target_pairs={{1,0},{2,1},{3,2},{4,3},{5,4},{6,5},{7,6},{8,7},{9,8},{10,9},{11,1... | collective-permute-start | bytes 491528 | tf_op jit(solution)/shard_map/ppermute | solution.py:489
  103.8 15.3 %collective-permute-start.9 = (f32[2,5,4,1024]{3,2,1,0:T(4,128)S(1)}, f32[2,5,4,1024]{3,2,1,0:T(4,128)S(1)}, u32[]{:S(2)}, u32[]{:S(2)}) collective-permute-start(f32[2,5,4,1024]{3,2,1,0:T(4,128)S(1)} %get-tuple-element.22), channel_id=1, source_target_pairs={{0,1},{1,2},{2,3},{3,4},{4,5},{5,6},{6,7},{7,8},{8,9},{9,10},{10,1... | collective-permute-start | bytes 491528 | tf_op jit(solution)/shard_map/ppermute | solution.py:489
